TPU v7x, 256 devices: a whole 4x4x8 slice. The times are simulated.
256 devices in a mesh: gx: 32 (over z, x_lo, core), gy: 8 (over y, x_hi).
Axes of the slice: x: 4 (x_hi: 2, x_lo: 2; x = x_hi * 2 + x_lo), y: 4, z: 8, core: 2. Of those that a mesh axis runs over, the one named last changes fastest.
Arguments:
- vectors: bfloat16 [128, 64, 128, 128], P('gx', 'gy'), may hold values from -6 to 6
- hamiltonian: bfloat16 [128, 64, 9, 128, 128], P('gx', 'gy'), may hold values from -0.125 to 0.125
- neighbours: int32 [128, 64, 9], P('gx', 'gy'), may hold values from 0 to 8, each once within a row
Outputs:
- filtered: float32 [128, 64, 128, 128], P('gx', 'gy')
Inputs may be any that keep to these rules, and one draw needn't show every extreme that they name: `neighbours`: each cell's list names every offset code 0 to 8 exactly once, in any order.
All inputs are finite; a program needn't handle non-finite values.
Results may differ from a plain program's by a relative error of at most 0.0034.
Values may be sent and summed in bfloat16 or wider, within the bound.
No kernel may reach another device: no remote copies, remote signals or barrier semaphores. Data moves between devices by JAX's collectives and lax.ppermute only.
A program may use at most 128 MiB of HBM per device.

v0:
```python
import jax
import jax.numpy as jnp
from jax import lax
from jax.sharding import PartitionSpec as P

STEPS = 4
NBR = 9


def padded_2(value, sides, width):
    for axis, dim in sides:
        size, length = (lax.axis_size(axis), value.shape[dim])
        up = [(i, (i + 1) % size) for i in range(size)]
        down = [(j, i) for i, j in up]
        last = lax.slice_in_dim(value, length - width, length, axis=dim)
        first = lax.slice_in_dim(value, 0, width, axis=dim)
        before = lax.ppermute(last, axis, up)
        after = lax.ppermute(first, axis, down)
        value = jnp.concatenate([before, value, after], axis=dim)
    return value


def neighbour_stack(padded, cell_rows, cell_cols):
    views = []
    for offset_x in (-1, 0, 1):
        for offset_y in (-1, 0, 1):
            views.append(
                padded[
                    1 + offset_x : 1 + offset_x + cell_rows, 1 + offset_y : 1 + offset_y + cell_cols
                ]
            )
    return jnp.stack(views, axis=0)


def on_device(vectors, hamiltonian, neighbours):
    cell_rows = vectors.shape[0]
    cell_cols = vectors.shape[1]
    onehot = (neighbours[..., None] == jnp.arange(NBR, dtype=jnp.int32)).astype(jnp.bfloat16)
    ordered = jnp.einsum(
        "xyko,xykij->xyoij", onehot, hamiltonian, preferred_element_type=jnp.float32
    ).astype(jnp.bfloat16)

    def operate(current_b):
        widened = padded_2(current_b, (("gx", 0),), 1)
        padded = padded_2(widened, (("gy", 1),), 1)
        stacked = neighbour_stack(padded, cell_rows, cell_cols)
        return jnp.einsum("xyoij,oxyjm->xyim", ordered, stacked, preferred_element_type=jnp.float32)

    previous = vectors.astype(jnp.float32)
    current = operate(vectors)
    for step_index in range(1, STEPS):
        following = 2.0 * operate(current.astype(jnp.bfloat16)) - previous
        previous = current
        current = following
    return current


def solution(mesh):
    placed = (P("gx", "gy", None, None), P("gx", "gy", None, None, None), P("gx", "gy", None))
    return jax.shard_map(
        on_device, mesh=mesh, in_specs=placed, out_specs=P("gx", "gy", None, None), check_vma=False
    )
```

profile of v0, /device:TPU:1, one launch (start us, length us, event | category | flops | bytes accessed | tf_op | source)
XLA Modules:
  0.0 173.8 jit_solution(4596129262267390978)
XLA Ops:
  0.0 1.2 fusion.75
  1.2 2.7 %collective-permute-start = (bf16[1,8,128,128]{3,2,1,0:T(8,128)(2,1)S(1)}, bf16[1,8,128,128]{3,2,1,0:T(8,128)(2,1)S(1)}, u32[]{:S(2)}, u32[]{:S(2)}) collective-permute-start(bf16[1,8,128,128]{3,2,1,0:T(8,128)(2,1)S(1)} %get-tuple-element.26), channel_id=1, source_target_pairs={{0,8},{8,16},{16,24},{24,32},{32,40},{40,48},{48,56},{56,64},{64,7... | collective-permute-start | bytes 786440 | tf_op jit(solution)/shard_map/ppermute | solution.py:17
  4.6 2.6 %collective-permute-done = bf16[1,8,128,128]{3,2,1,0:T(8,128)(2,1)S(1)} collective-permute-done((bf16[1,8,128,128]{3,2,1,0:T(8,128)(2,1)S(1)}, bf16[1,8,128,128]{3,2,1,0:T(8,128)(2,1)S(1)}, u32[]{:S(2)}, u32[]{:S(2)}) %collective-permute-start) | collective-permute-done | bytes 262176 | tf_op jit(solution)/shard_map/ppermute | solution.py:17
  7.4 5.3 %collective-permute-done.1 = bf16[1,8,128,128]{3,2,1,0:T(8,128)(2,1)S(1)} collective-permute-done((bf16[1,8,128,128]{3,2,1,0:T(8,128)(2,1)S(1)}, bf16[1,8,128,128]{3,2,1,0:T(8,128)(2,1)S(1)}, u32[]{:S(2)}, u32[]{:S(2)}) %collective-permute-start.1) | collective-permute-done | bytes 262176 | tf_op jit(solution)/shard_map/ppermute | solution.py:18
  12.8 2.5 %collective-permute-start.2 = (bf16[6,1,128,128]{3,2,1,0:T(8,128)(2,1)S(1)}, bf16[6,1,128,128]{3,2,1,0:T(8,128)(2,1)S(1)}, u32[]{:S(2)}, u32[]{:S(2)}) collective-permute-start(bf16[6,1,128,128]{3,2,1,0:T(8,128)(2,1)S(1)} %get-tuple-element.18), channel_id=1, source_target_pairs={{0,1},{1,2},{2,3},{3,4},{4,5},{5,6},{6,7},{7,0},{8,9},{9,10},{10,1... | collective-permute-start | bytes 589832 | tf_op jit(solution)/shard_map/ppermute | solution.py:17
  15.3 13.4 %fusion = bf16[4,8,9,128,128]{4,2,3,1,0:T(8,128)(2,1)} fusion(bf16[4,8,9,128,128]{4,3,2,1,0:T(8,128)(2,1)} %param.4, s32[4,8,9]{2,1,0:T(8,128)S(1)} %copy-done.3), kind=kOutput, calls=%fused_computation.1 | convolution fusion | flops 84937248 | bytes 18875520 | tf_op jit(solution)/shard_map/xyko,xykij->xyoij/dot_general | solution.py:39
  28.7 8.1 %copy.47 = bf16[4,8,9,128,128]{4,3,2,1,0:T(8,128)(2,1)S(1)} copy(bf16[4,8,9,128,128]{4,2,3,1,0:T(8,128)(2,1)} %fusion) | data formatting | bytes 18874368 | tf_op jit(solution)/shard_map/xyko,xykij->xyoij/dot_general | solution.py:39
  36.8 2.9 %collective-permute-start.3 = (bf16[6,1,128,128]{3,2,1,0:T(8,128)(2,1)S(1)}, bf16[6,1,128,128]{3,2,1,0:T(8,128)(2,1)S(1)}, u32[]{:S(2)}, u32[]{:S(2)}) collective-permute-start(bf16[6,1,128,128]{3,2,1,0:T(8,128)(2,1)S(1)} %get-tuple-element.17), channel_id=1, source_target_pairs={{1,0},{2,1},{3,2},{4,3},{5,4},{6,5},{7,6},{0,7},{9,8},{10,9},{11,1... | collective-permute-start | bytes 589832 | tf_op jit(solution)/shard_map/ppermute | solution.py:18
  39.7 1.2 fusion.29
  40.9 1.2 fusion.67
  42.1 1.9 %collective-permute-done.3 = bf16[6,1,128,128]{3,2,1,0:T(8,128)(2,1)S(1)} collective-permute-done((bf16[6,1,128,128]{3,2,1,0:T(8,128)(2,1)S(1)}, bf16[6,1,128,128]{3,2,1,0:T(8,128)(2,1)S(1)}, u32[]{:S(2)}, u32[]{:S(2)}) %collective-permute-start.3) | collective-permute-done | bytes 196640 | tf_op jit(solution)/shard_map/ppermute | solution.py:18
  44.0 1.2 fusion.23
  45.2 1.2 fusion.26
  46.4 1.2 bitcast_dynamic-update-slice_fusion.3
  47.6 1.2 fusion.20
  48.8 1.2 fusion.65
  50.0 1.2 fusion.63
  51.2 1.2 fusion.61
  52.4 7.7 %bitcast_convert_fusion = (bf16[4,8,128,128]{3,2,1,0:T(8,128)(2,1)S(1)}, f32[4,8,128,128,1]{3,2,4,1,0:T(8,128)}) fusion(bf16[4,8,9,128,128]{4,3,2,1,0:T(8,128)(2,1)S(1)} %copy.47, bf16[9,4,8,128,128]{4,3,0,2,1:T(8,128)(2,1)} %fusion.61), kind=kOutput, calls=%fused_computation.20 | convolution fusion | flops 1208483840 | bytes 22020096 | tf_op jit(solution)/shard_map/xyoij,oxyjm->xyim/dot_general | solution.py:47
  60.2 1.9 %collective-permute-start.5 = (bf16[1,8,128,128]{3,2,1,0:T(8,128)(2,1)S(1)}, bf16[1,8,128,128]{3,2,1,0:T(8,128)(2,1)S(1)}, u32[]{:S(2)}, u32[]{:S(2)}) collective-permute-start(bf16[1,8,128,128]{3,2,1,0:T(8,128)(2,1)S(1)} %get-tuple-element.24), channel_id=1, source_target_pairs={{8,0},{16,8},{24,16},{32,24},{40,32},{48,40},{56,48},{64,56},{72,6... | collective-permute-start | bytes 786440 | tf_op jit(solution)/shard_map/ppermute | solution.py:18
  62.1 1.4 collective-permute-done.4
  63.5 2.6 %collective-permute-done.5 = bf16[1,8,128,128]{3,2,1,0:T(8,128)(2,1)S(1)} collective-permute-done((bf16[1,8,128,128]{3,2,1,0:T(8,128)(2,1)S(1)}, bf16[1,8,128,128]{3,2,1,0:T(8,128)(2,1)S(1)}, u32[]{:S(2)}, u32[]{:S(2)}) %collective-permute-start.5) | collective-permute-done | bytes 262176 | tf_op jit(solution)/shard_map/ppermute | solution.py:18
  66.1 4.8 %collective-permute-start.7 = (bf16[6,1,128,128]{3,2,1,0:T(8,128)(2,1)S(1)}, bf16[6,1,128,128]{3,2,1,0:T(8,128)(2,1)S(1)}, u32[]{:S(2)}, u32[]{:S(2)}) collective-permute-start(bf16[6,1,128,128]{3,2,1,0:T(8,128)(2,1)S(1)} %get-tuple-element.15), channel_id=1, source_target_pairs={{1,0},{2,1},{3,2},{4,3},{5,4},{6,5},{7,6},{0,7},{9,8},{10,9},{11,1... | collective-permute-start | bytes 589832 | tf_op jit(solution)/shard_map/ppermute | solution.py:18
  70.9 2.6 %collective-permute-done.7 = bf16[6,1,128,128]{3,2,1,0:T(8,128)(2,1)S(1)} collective-permute-done((bf16[6,1,128,128]{3,2,1,0:T(8,128)(2,1)S(1)}, bf16[6,1,128,128]{3,2,1,0:T(8,128)(2,1)S(1)}, u32[]{:S(2)}, u32[]{:S(2)}) %collective-permute-start.7) | collective-permute-done | bytes 196640 | tf_op jit(solution)/shard_map/ppermute | solution.py:18
  73.6 7.6 %collective-permute-done.6 = bf16[6,1,128,128]{3,2,1,0:T(8,128)(2,1)S(1)} collective-permute-done((bf16[6,1,128,128]{3,2,1,0:T(8,128)(2,1)S(1)}, bf16[6,1,128,128]{3,2,1,0:T(8,128)(2,1)S(1)}, u32[]{:S(2)}, u32[]{:S(2)}) %collective-permute-start.6) | collective-permute-done | bytes 196640 | tf_op jit(solution)/shard_map/ppermute | solution.py:17
  83.8 1.1 fusion.56
  91.2 7.9 %fusion.76 = (bf16[4,8,128,128]{3,2,1,0:T(8,128)(2,1)S(1)}, f32[4,8,128,128]{3,2,1,0:T(8,128)}) fusion(bf16[4,8,128,128]{3,2,1,0:T(8,128)(2,1)S(1)} %copy-done.1, bf16[4,8,9,128,128]{4,3,2,1,0:T(8,128)(2,1)S(1)} %bitcast.178, bf16[9,4,8,128,128]{4,3,2,1,0:T(8,128)(2,1)} %fusion.50), kind=kOutput, calls=%fused_computation.133 | convolution fusion | flops 1210056704 | bytes 23068672 | tf_op jit(solution)/shard_map/xyoij,oxyjm->xyim/dot_general | solution.py:47
  99.1 2.5 %collective-permute-start.8 = (bf16[1,8,128,128]{3,2,1,0:T(8,128)(2,1)S(1)}, bf16[1,8,128,128]{3,2,1,0:T(8,128)(2,1)S(1)}, u32[]{:S(2)}, u32[]{:S(2)}) collective-permute-start(bf16[1,8,128,128]{3,2,1,0:T(8,128)(2,1)S(1)} %get-tuple-element.21), channel_id=1, source_target_pairs={{0,8},{8,16},{16,24},{24,32},{32,40},{40,48},{48,56},{56,64},{64,7... | collective-permute-start | bytes 786440 | tf_op jit(solution)/shard_map/ppermute | solution.py:17
  101.6 1.1 collective-permute-start.9
  102.7 5.0 %collective-permute-done.8 = bf16[1,8,128,128]{3,2,1,0:T(8,128)(2,1)S(1)} collective-permute-done((bf16[1,8,128,128]{3,2,1,0:T(8,128)(2,1)S(1)}, bf16[1,8,128,128]{3,2,1,0:T(8,128)(2,1)S(1)}, u32[]{:S(2)}, u32[]{:S(2)}) %collective-permute-start.8) | collective-permute-done | bytes 262176 | tf_op jit(solution)/shard_map/ppermute | solution.py:17
  107.7 2.6 %collective-permute-done.9 = bf16[1,8,128,128]{3,2,1,0:T(8,128)(2,1)S(1)} collective-permute-done((bf16[1,8,128,128]{3,2,1,0:T(8,128)(2,1)S(1)}, bf16[1,8,128,128]{3,2,1,0:T(8,128)(2,1)S(1)}, u32[]{:S(2)}, u32[]{:S(2)}) %collective-permute-start.9) | collective-permute-done | bytes 262176 | tf_op jit(solution)/shard_map/ppermute | solution.py:18
  110.4 1.7 collective-permute-start.11
  112.1 1.3 collective-permute-start.10
  113.5 4.7 %collective-permute-done.11 = bf16[6,1,128,128]{3,2,1,0:T(8,128)(2,1)S(1)} collective-permute-done((bf16[6,1,128,128]{3,2,1,0:T(8,128)(2,1)S(1)}, bf16[6,1,128,128]{3,2,1,0:T(8,128)(2,1)S(1)}, u32[]{:S(2)}, u32[]{:S(2)}) %collective-permute-start.11) | collective-permute-done | bytes 196640 | tf_op jit(solution)/shard_map/ppermute | solution.py:18
  118.2 4.2 %collective-permute-done.10 = bf16[6,1,128,128]{3,2,1,0:T(8,128)(2,1)S(1)} collective-permute-done((bf16[6,1,128,128]{3,2,1,0:T(8,128)(2,1)S(1)}, bf16[6,1,128,128]{3,2,1,0:T(8,128)(2,1)S(1)}, u32[]{:S(2)}, u32[]{:S(2)}) %collective-permute-start.10) | collective-permute-done | bytes 196640 | tf_op jit(solution)/shard_map/ppermute | solution.py:17
  124.0 1.1 fusion.48
  125.1 1.1 fusion.46
  128.3 1.1 fusion.44
  129.5 1.1 fusion.43
  130.6 1.1 fusion.42
  132.7 7.1 %fusion.10 = bf16[4,8,128,128]{3,2,1,0:T(8,128)(2,1)S(1)} fusion(f32[4,8,128,128,1]{3,2,4,1,0:T(8,128)} %get-tuple-element.28, bf16[4,8,9,128,128]{4,3,2,1,0:T(8,128)(2,1)S(1)} %bitcast.178, bf16[9,4,8,128,128]{4,3,2,1,0:T(8,128)(2,1)} %fusion.40), kind=kOutput, calls=%fused_computation.17 | convolution fusion | flops 1209532416 | bytes 22020096 | tf_op jit(solution)/shard_map/xyoij,oxyjm->xyim/dot_general | solution.py:47
  140.7 4.9 %collective-permute-done.12 = bf16[1,8,128,128]{3,2,1,0:T(8,128)(2,1)S(1)} collective-permute-done((bf16[1,8,128,128]{3,2,1,0:T(8,128)(2,1)S(1)}, bf16[1,8,128,128]{3,2,1,0:T(8,128)(2,1)S(1)}, u32[]{:S(2)}, u32[]{:S(2)}) %collective-permute-start.12) | collective-permute-done | bytes 262176 | tf_op jit(solution)/shard_map/ppermute | solution.py:17
  145.5 3.7 %collective-permute-done.13 = bf16[1,8,128,128]{3,2,1,0:T(8,128)(2,1)S(1)} collective-permute-done((bf16[1,8,128,128]{3,2,1,0:T(8,128)(2,1)S(1)}, bf16[1,8,128,128]{3,2,1,0:T(8,128)(2,1)S(1)}, u32[]{:S(2)}, u32[]{:S(2)}) %collective-permute-start.13) | collective-permute-done | bytes 262176 | tf_op jit(solution)/shard_map/ppermute | solution.py:18
  149.4 3.0 %collective-permute-start.14 = (bf16[6,1,128,128]{3,2,1,0:T(8,128)(2,1)S(1)}, bf16[6,1,128,128]{3,2,1,0:T(8,128)(2,1)S(1)}, u32[]{:S(2)}, u32[]{:S(2)}) collective-permute-start(bf16[6,1,128,128]{3,2,1,0:T(8,128)(2,1)S(1)} %get-tuple-element.8), channel_id=1, source_target_pairs={{0,1},{1,2},{2,3},{3,4},{4,5},{5,6},{6,7},{7,0},{8,9},{9,10},{10,1... | collective-permute-start | bytes 589832 | tf_op jit(solution)/shard_map/ppermute | solution.py:17
  152.3 5.5 %collective-permute-done.15 = bf16[6,1,128,128]{3,2,1,0:T(8,128)(2,1)S(1)} collective-permute-done((bf16[6,1,128,128]{3,2,1,0:T(8,128)(2,1)S(1)}, bf16[6,1,128,128]{3,2,1,0:T(8,128)(2,1)S(1)}, u32[]{:S(2)}, u32[]{:S(2)}) %collective-permute-start.15) | collective-permute-done | bytes 196640 | tf_op jit(solution)/shard_map/ppermute | solution.py:18
  157.8 2.1 %collective-permute-done.14 = bf16[6,1,128,128]{3,2,1,0:T(8,128)(2,1)S(1)} collective-permute-done((bf16[6,1,128,128]{3,2,1,0:T(8,128)(2,1)S(1)}, bf16[6,1,128,128]{3,2,1,0:T(8,128)(2,1)S(1)}, u32[]{:S(2)}, u32[]{:S(2)}) %collective-permute-start.14) | collective-permute-done | bytes 196640 | tf_op jit(solution)/shard_map/ppermute | solution.py:17
  161.8 3.7 %copy-done.2 = bf16[9,4,8,128,128]{4,3,2,1,0:T(8,128)(2,1)} copy-done((bf16[9,4,8,128,128]{4,3,2,1,0:T(8,128)(2,1)}, bf16[9,4,8,128,128]{4,3,2,1,0:T(8,128)(2,1)S(1)}, u32[]{:S(2)}) %copy-start.2) | copy-done | bytes 9437208
  165.4 8.4 %fusion.8 = f32[4,8,128,128]{3,2,1,0:T(8,128)} fusion(f32[4,8,128,128]{3,2,1,0:T(8,128)} %get-tuple-element.30, bf16[4,8,9,128,128]{4,3,2,1,0:T(8,128)(2,1)S(1)} %bitcast.178, bf16[9,4,8,128,128]{4,3,2,1,0:T(8,128)(2,1)} %copy-done.2), kind=kOutput, calls=%fused_computation.14 | convolution fusion | flops 1209008128 | bytes 23068672 | tf_op jit(solution)/shard_map/xyoij,oxyjm->xyim/dot_general | solution.py:47
  (55 shorter events, 17.8 us)
Async XLA Ops:
  0.0 7.2 %copy-start.1 = (bf16[4,8,128,128]{3,2,1,0:T(8,128)(2,1)S(1)}, bf16[4,8,128,128]{3,2,1,0:T(8,128)(2,1)}, u32[]{:S(2)}) copy-start(bf16[4,8,128,128]{3,2,1,0:T(8,128)(2,1)} %param.3) | copy-start | bytes 3145732
  1.2 14.1 %copy-start.3 = (s32[4,8,9]{2,1,0:T(8,128)S(1)}, s32[4,8,9]{2,1,0:T(8,128)}, u32[]{:S(2)}) copy-start(s32[4,8,9]{2,1,0:T(8,128)} %param.5) | copy-start | bytes 3460
  1.2 6.0 %collective-permute-start = (bf16[1,8,128,128]{3,2,1,0:T(8,128)(2,1)S(1)}, bf16[1,8,128,128]{3,2,1,0:T(8,128)(2,1)S(1)}, u32[]{:S(2)}, u32[]{:S(2)}) collective-permute-start(bf16[1,8,128,128]{3,2,1,0:T(8,128)(2,1)S(1)} %get-tuple-element.26), channel_id=1, source_target_pairs={{0,8},{8,16},{16,24},{24,32},{32,40},{40,48},{48,56},{56,64},{64,7... | collective-permute-start | bytes 786440 | tf_op jit(solution)/shard_map/ppermute | solution.py:17
  3.9 8.8 %collective-permute-start.1 = (bf16[1,8,128,128]{3,2,1,0:T(8,128)(2,1)S(1)}, bf16[1,8,128,128]{3,2,1,0:T(8,128)(2,1)S(1)}, u32[]{:S(2)}, u32[]{:S(2)}) collective-permute-start(bf16[1,8,128,128]{3,2,1,0:T(8,128)(2,1)S(1)} %get-tuple-element.25), channel_id=1, source_target_pairs={{8,0},{16,8},{24,16},{32,24},{40,32},{48,40},{56,48},{64,56},{72,6... | collective-permute-start | bytes 786440 | tf_op jit(solution)/shard_map/ppermute | solution.py:18
  12.8 26.9 %collective-permute-start.2 = (bf16[6,1,128,128]{3,2,1,0:T(8,128)(2,1)S(1)}, bf16[6,1,128,128]{3,2,1,0:T(8,128)(2,1)S(1)}, u32[]{:S(2)}, u32[]{:S(2)}) collective-permute-start(bf16[6,1,128,128]{3,2,1,0:T(8,128)(2,1)S(1)} %get-tuple-element.18), channel_id=1, source_target_pairs={{0,1},{1,2},{2,3},{3,4},{4,5},{5,6},{6,7},{7,0},{8,9},{9,10},{10,1... | collective-permute-start | bytes 589832 | tf_op jit(solution)/shard_map/ppermute | solution.py:17
  36.8 15.6 %copy-start = (bf16[4,8,9,128,128]{4,3,2,1,0:T(8,128)(2,1)}, bf16[4,8,9,128,128]{4,3,2,1,0:T(8,128)(2,1)S(1)}, u32[]{:S(2)}) copy-start(bf16[4,8,9,128,128]{4,3,2,1,0:T(8,128)(2,1)S(1)} %copy.47) | copy-start | bytes 28311556
  36.8 7.2 %collective-permute-start.3 = (bf16[6,1,128,128]{3,2,1,0:T(8,128)(2,1)S(1)}, bf16[6,1,128,128]{3,2,1,0:T(8,128)(2,1)S(1)}, u32[]{:S(2)}, u32[]{:S(2)}) collective-permute-start(bf16[6,1,128,128]{3,2,1,0:T(8,128)(2,1)S(1)} %get-tuple-element.17), channel_id=1, source_target_pairs={{1,0},{2,1},{3,2},{4,3},{5,4},{6,5},{7,6},{0,7},{9,8},{10,9},{11,1... | collective-permute-start | bytes 589832 | tf_op jit(solution)/shard_map/ppermute | solution.py:18
  60.1 3.4 %collective-permute-start.4 = (bf16[1,8,128,128]{3,2,1,0:T(8,128)(2,1)S(1)}, bf16[1,8,128,128]{3,2,1,0:T(8,128)(2,1)S(1)}, u32[]{:S(2)}, u32[]{:S(2)}) collective-permute-start(bf16[1,8,128,128]{3,2,1,0:T(8,128)(2,1)S(1)} %get-tuple-element.23), channel_id=1, source_target_pairs={{0,8},{8,16},{16,24},{24,32},{32,40},{40,48},{48,56},{56,64},{64,7... | collective-permute-start | bytes 786440 | tf_op jit(solution)/shard_map/ppermute | solution.py:17
  60.2 5.9 %collective-permute-start.5 = (bf16[1,8,128,128]{3,2,1,0:T(8,128)(2,1)S(1)}, bf16[1,8,128,128]{3,2,1,0:T(8,128)(2,1)S(1)}, u32[]{:S(2)}, u32[]{:S(2)}) collective-permute-start(bf16[1,8,128,128]{3,2,1,0:T(8,128)(2,1)S(1)} %get-tuple-element.24), channel_id=1, source_target_pairs={{8,0},{16,8},{24,16},{32,24},{40,32},{48,40},{56,48},{64,56},{72,6... | collective-permute-start | bytes 786440 | tf_op jit(solution)/shard_map/ppermute | solution.py:18
  66.1 7.4 %collective-permute-start.7 = (bf16[6,1,128,128]{3,2,1,0:T(8,128)(2,1)S(1)}, bf16[6,1,128,128]{3,2,1,0:T(8,128)(2,1)S(1)}, u32[]{:S(2)}, u32[]{:S(2)}) collective-permute-start(bf16[6,1,128,128]{3,2,1,0:T(8,128)(2,1)S(1)} %get-tuple-element.15), channel_id=1, source_target_pairs={{1,0},{2,1},{3,2},{4,3},{5,4},{6,5},{7,6},{0,7},{9,8},{10,9},{11,1... | collective-permute-start | bytes 589832 | tf_op jit(solution)/shard_map/ppermute | solution.py:18
  70.9 10.2 %collective-permute-start.6 = (bf16[6,1,128,128]{3,2,1,0:T(8,128)(2,1)S(1)}, bf16[6,1,128,128]{3,2,1,0:T(8,128)(2,1)S(1)}, u32[]{:S(2)}, u32[]{:S(2)}) collective-permute-start(bf16[6,1,128,128]{3,2,1,0:T(8,128)(2,1)S(1)} %get-tuple-element.16), channel_id=1, source_target_pairs={{0,1},{1,2},{2,3},{3,4},{4,5},{5,6},{6,7},{7,0},{8,9},{9,10},{10,1... | collective-permute-start | bytes 589832 | tf_op jit(solution)/shard_map/ppermute | solution.py:17
  81.1 10.1 %slice-start = ((s8[9437184]{0:T(1024)(128)(4,1)}), s8[4194304]{0:T(1024)(128)(4,1)S(1)}, s32[]{:S(2)}) async-start(s8[9437184]{0:T(1024)(128)(4,1)} %bitcast.177), calls=%async_computation | async-start | bytes 8388608
  82.7 8.5 %slice-start.1 = ((s8[9437184]{0:T(1024)(128)(4,1)}), s8[4194304]{0:T(1024)(128)(4,1)S(1)}, s32[]{:S(2)}) async-start(s8[9437184]{0:T(1024)(128)(4,1)} %bitcast.177), calls=%async_computation.1 | async-start | bytes 8388608
  87.0 4.2 %slice-start.2 = ((s8[9437184]{0:T(1024)(128)(4,1)}), s8[1048576]{0:T(1024)(128)(4,1)S(1)}, s32[]{:S(2)}) async-start(s8[9437184]{0:T(1024)(128)(4,1)} %bitcast.177), calls=%async_computation.2 | async-start | bytes 2097152
  99.1 8.6 %collective-permute-start.8 = (bf16[1,8,128,128]{3,2,1,0:T(8,128)(2,1)S(1)}, bf16[1,8,128,128]{3,2,1,0:T(8,128)(2,1)S(1)}, u32[]{:S(2)}, u32[]{:S(2)}) collective-permute-start(bf16[1,8,128,128]{3,2,1,0:T(8,128)(2,1)S(1)} %get-tuple-element.21), channel_id=1, source_target_pairs={{0,8},{8,16},{16,24},{24,32},{32,40},{40,48},{48,56},{56,64},{64,7... | collective-permute-start | bytes 786440 | tf_op jit(solution)/shard_map/ppermute | solution.py:17
  101.6 8.8 %collective-permute-start.9 = (bf16[1,8,128,128]{3,2,1,0:T(8,128)(2,1)S(1)}, bf16[1,8,128,128]{3,2,1,0:T(8,128)(2,1)S(1)}, u32[]{:S(2)}, u32[]{:S(2)}) collective-permute-start(bf16[1,8,128,128]{3,2,1,0:T(8,128)(2,1)S(1)} %get-tuple-element.22), channel_id=1, source_target_pairs={{8,0},{16,8},{24,16},{32,24},{40,32},{48,40},{56,48},{64,56},{72,6... | collective-permute-start | bytes 786440 | tf_op jit(solution)/shard_map/ppermute | solution.py:18
  110.4 7.8 %collective-permute-start.11 = (bf16[6,1,128,128]{3,2,1,0:T(8,128)(2,1)S(1)}, bf16[6,1,128,128]{3,2,1,0:T(8,128)(2,1)S(1)}, u32[]{:S(2)}, u32[]{:S(2)}) collective-permute-start(bf16[6,1,128,128]{3,2,1,0:T(8,128)(2,1)S(1)} %get-tuple-element.11), channel_id=1, source_target_pairs={{1,0},{2,1},{3,2},{4,3},{5,4},{6,5},{7,6},{0,7},{9,8},{10,9},{11,1... | collective-permute-start | bytes 589832 | tf_op jit(solution)/shard_map/ppermute | solution.py:18
  112.1 10.3 %collective-permute-start.10 = (bf16[6,1,128,128]{3,2,1,0:T(8,128)(2,1)S(1)}, bf16[6,1,128,128]{3,2,1,0:T(8,128)(2,1)S(1)}, u32[]{:S(2)}, u32[]{:S(2)}) collective-permute-start(bf16[6,1,128,128]{3,2,1,0:T(8,128)(2,1)S(1)} %get-tuple-element.12), channel_id=1, source_target_pairs={{0,1},{1,2},{2,3},{3,4},{4,5},{5,6},{6,7},{7,0},{8,9},{9,10},{10,1... | collective-permute-start | bytes 589832 | tf_op jit(solution)/shard_map/ppermute | solution.py:17
  139.8 5.7 %collective-permute-start.12 = (bf16[1,8,128,128]{3,2,1,0:T(8,128)(2,1)S(1)}, bf16[1,8,128,128]{3,2,1,0:T(8,128)(2,1)S(1)}, u32[]{:S(2)}, u32[]{:S(2)}) collective-permute-start(bf16[1,8,128,128]{3,2,1,0:T(8,128)(2,1)S(1)} %get-tuple-element.19), channel_id=1, source_target_pairs={{0,8},{8,16},{16,24},{24,32},{32,40},{40,48},{48,56},{56,64},{64,7... | collective-permute-start | bytes 786440 | tf_op jit(solution)/shard_map/ppermute | solution.py:17
  139.9 9.3 %collective-permute-start.13 = (bf16[1,8,128,128]{3,2,1,0:T(8,128)(2,1)S(1)}, bf16[1,8,128,128]{3,2,1,0:T(8,128)(2,1)S(1)}, u32[]{:S(2)}, u32[]{:S(2)}) collective-permute-start(bf16[1,8,128,128]{3,2,1,0:T(8,128)(2,1)S(1)} %get-tuple-element.20), channel_id=1, source_target_pairs={{8,0},{16,8},{24,16},{32,24},{40,32},{48,40},{56,48},{64,56},{72,6... | collective-permute-start | bytes 786440 | tf_op jit(solution)/shard_map/ppermute | solution.py:18
  149.3 8.5 %collective-permute-start.15 = (bf16[6,1,128,128]{3,2,1,0:T(8,128)(2,1)S(1)}, bf16[6,1,128,128]{3,2,1,0:T(8,128)(2,1)S(1)}, u32[]{:S(2)}, u32[]{:S(2)}) collective-permute-start(bf16[6,1,128,128]{3,2,1,0:T(8,128)(2,1)S(1)} %get-tuple-element.7), channel_id=1, source_target_pairs={{1,0},{2,1},{3,2},{4,3},{5,4},{6,5},{7,6},{0,7},{9,8},{10,9},{11,1... | collective-permute-start | bytes 589832 | tf_op jit(solution)/shard_map/ppermute | solution.py:18
  149.4 10.5 %collective-permute-start.14 = (bf16[6,1,128,128]{3,2,1,0:T(8,128)(2,1)S(1)}, bf16[6,1,128,128]{3,2,1,0:T(8,128)(2,1)S(1)}, u32[]{:S(2)}, u32[]{:S(2)}) collective-permute-start(bf16[6,1,128,128]{3,2,1,0:T(8,128)(2,1)S(1)} %get-tuple-element.8), channel_id=1, source_target_pairs={{0,1},{1,2},{2,3},{3,4},{4,5},{5,6},{6,7},{7,0},{8,9},{9,10},{10,1... | collective-permute-start | bytes 589832 | tf_op jit(solution)/shard_map/ppermute | solution.py:17
  161.7 3.7 %copy-start.2 = (bf16[9,4,8,128,128]{4,3,2,1,0:T(8,128)(2,1)}, bf16[9,4,8,128,128]{4,3,2,1,0:T(8,128)(2,1)S(1)}, u32[]{:S(2)}) copy-start(bf16[9,4,8,128,128]{4,3,2,1,0:T(8,128)(2,1)S(1)} %fusion.30) | copy-start | bytes 28311556
where the time goes:
time: 176 us; the launch traced here: 174 us
  waiting for transfers between devices  56.6 us (32%)
  matrix products  44.4 us (25%)
  local copies, waits for them, and re-layouts  30.3 us (17%)
  starting transfers between devices  26.2 us (15%)
  other arithmetic  16 us (9%)
    dot_general x4, matrix products, operate(): jnp.einsum('xyoij,oxyjm->xyim', ordered, stacked, preferred_element_type=...  31 us
    ppermute x8, waiting for transfers between devices, padded_2(): after = lax.ppermute(first, axis, down)  28.9 us
    ppermute x8, waiting for transfers between devices, padded_2(): before = lax.ppermute(last, axis, up)  27.7 us
    unnamed x35, local copies, waits for them, and re-layouts  18.7 us
    ppermute x8, starting transfers between devices, padded_2(): after = lax.ppermute(first, axis, down)  14 us
    dot_general x1, matrix products, on_device(): jnp.einsum('xyko,xykij->xyoij', onehot, hamiltonian, preferred_element_ty...  13.4 us
    unnamed x14, other arithmetic  13 us
    ppermute x8, starting transfers between devices, padded_2(): before = lax.ppermute(last, axis, up)  12.2 us
  transfers between devices with their start and end apart: 16, of which 15 were waited for; matrix products, arithmetic and copies ran while one was open for 14% of the time, Pallas kernels for 0%

commit v1 on v0

v1 whole, which is shorter than its diff:
```python
import functools

import jax
import jax.numpy as jnp
from jax import lax
from jax.experimental import pallas as pl
from jax.experimental.pallas import tpu as pltpu
from jax.sharding import PartitionSpec as P

STEPS = 4
NBR = 9
VMEM = pl.BlockSpec(memory_space=pltpu.VMEM)
SMEM = pl.BlockSpec(memory_space=pltpu.SMEM)
LIMIT = 24 * 1024 * 1024


def product(blocks, fields):
    terms = [jnp.dot(h, v, preferred_element_type=jnp.float32) for h, v in zip(blocks, fields)]
    return functools.reduce(jnp.add, terms)


def local_kernel(first, rows, cols, *refs):
    if first:
        place, ham, field, total, rounded = refs
    else:
        place, ham, field, before, total, rounded = refs

    def cell(i, j, offsets_x, offsets_y, inside):
        codes = [(a, b) for a in offsets_x for b in offsets_y]
        blocks = [ham[i, j, place[(i * cols + j) * NBR + (a + 1) * 3 + b + 1]] for a, b in codes]
        value = product(blocks, [field[i + a, j + b] for a, b in codes])
        if not first:
            value = 2.0 * value - before[i, j].astype(jnp.float32)
        total[i, j] = value
        if inside:
            rounded[i, j] = value.astype(jnp.bfloat16)

    for i in range(rows):
        for j in range(cols):
            offsets_x = [a for a in (-1, 0, 1) if 0 <= i + a < rows]
            offsets_y = [b for b in (-1, 0, 1) if 0 <= j + b < cols]
            cell(i, j, offsets_x, offsets_y, len(offsets_x) * len(offsets_y) == NBR)


def rim_kernel(first, last, rows, cols, *refs):
    place, side, ham, near, far, even, odd, near2, far_even, far_odd, partial = refs[:11]
    if last:
        total, halo = refs[11:]
    else:
        total, rounded, *sends, halo = refs[12:]
    core, parity = side[0], side[1]
    row_near, row_far = (1 - core) * (rows + 1), core * (rows + 1)
    col_even, col_odd = (1 - parity) * (cols + 1), parity * (cols + 1)
    for j in range(cols):
        halo[row_near, j + 1] = near[j]
        halo[row_far, j + 1] = far[j]
    for i in range(rows):
        halo[i + 1, col_even] = even[i]
        halo[i + 1, col_odd] = odd[i]
    halo[row_near, col_even] = near2[0]
    halo[row_near, col_odd] = near2[1]
    halo[row_far, col_even] = far_even[...]
    halo[row_far, col_odd] = far_odd[...]

    for i in range(rows):
        for j in range(cols):
            codes = [
                (a, b)
                for a in (-1, 0, 1)
                for b in (-1, 0, 1)
                if not (0 <= i + a < rows and 0 <= j + b < cols)
            ]
            if codes:
                blocks = [ham[i, j, place[(i * cols + j) * NBR + (a + 1) * 3 + b + 1]] for a, b in codes]
                value = product(blocks, [halo[i + 1 + a, j + 1 + b] for a, b in codes])
                value = partial[i, j] + (value if first else 2.0 * value)
                total[i, j] = value
                if not last:
                    rounded[i, j] = value.astype(jnp.bfloat16)
            elif last:
                total[i, j] = partial[i, j]
    if not last:
        fill_edges(rounded, core, parity, rows, cols, *sends)


def fill_edges(field, core, parity, rows, cols, near, far, even, odd, far_even, far_odd):
    row_near, row_far = (1 - core) * (rows - 1), core * (rows - 1)
    col_even, col_odd = (1 - parity) * (cols - 1), parity * (cols - 1)
    for j in range(cols):
        near[j] = field[row_near, j]
        far[j] = field[row_far, j]
    for i in range(rows):
        even[i] = field[i, col_even]
        odd[i] = field[i, col_odd]
    far_even[...] = field[row_far, col_even]
    far_odd[...] = field[row_far, col_odd]


def edge_kernel(rows, cols, side, field, *sends):
    fill_edges(field, side[0], side[1], rows, cols, *sends)


def swaps(size_x, size_y):
    def pairs(move):
        out = []
        for x in range(size_x):
            for y in range(size_y):
                a, b = move(x, y)
                out.append((x * size_y + y, (a % size_x) * size_y + b % size_y))
        return out

    near = pairs(lambda x, y: (x ^ 1, y))
    far = pairs(lambda x, y: (x - 1 + 2 * (x % 2), y))
    even = pairs(lambda x, y: (x, y ^ 1))
    odd = pairs(lambda x, y: (x, y - 1 + 2 * (y % 2)))
    far_even = pairs(lambda x, y: (x - 1 + 2 * (x % 2), y ^ 1))
    far_odd = pairs(lambda x, y: (x - 1 + 2 * (x % 2), y - 1 + 2 * (y % 2)))
    return near, far, even, odd, far_even, far_odd


def on_device(vectors, hamiltonian, neighbours):
    rows, cols, size, trials = vectors.shape
    axes = ("gx", "gy")
    pairs = swaps(lax.axis_size("gx"), lax.axis_size("gy"))
    core = lax.axis_index("gx") % 2
    parity = lax.axis_index("gy") % 2
    side = jnp.stack([core, parity]).astype(jnp.int32)
    codes = jnp.arange(NBR, dtype=jnp.int32)
    hit = neighbours[:, :, None, :] == codes[:, None]
    place = jnp.sum(jnp.where(hit, codes, 0), axis=-1, dtype=jnp.int32).reshape(-1)

    def shape(*dims, dtype=jnp.bfloat16):
        return jax.ShapeDtypeStruct((*dims, size, trials), dtype)

    sends = (shape(cols), shape(cols), shape(rows), shape(rows), shape(), shape())
    params = pltpu.CompilerParams(vmem_limit_bytes=LIMIT)

    def cost(products):
        return pl.CostEstimate(flops=products * 2 * size * size * trials, bytes_accessed=products * 2 * size * size, transcendentals=0)

    edges = pl.pallas_call(
        functools.partial(edge_kernel, rows, cols),
        out_shape=sends,
        in_specs=[SMEM, VMEM],
        out_specs=[VMEM] * len(sends),
        compiler_params=params,
        name="edges",
    )(side, vectors)

    def travel(edges):
        near, far, even, odd, far_even, far_odd = [
            lax.ppermute(sent, axes, pair) for sent, pair in zip(edges, pairs)
        ]
        row_near = (1 - core) * (rows - 1)
        both = jnp.stack([lax.dynamic_index_in_dim(v, row_near, keepdims=False) for v in (even, odd)])
        near2 = lax.ppermute(both, axes, pairs[0])
        return near, far, even, odd, near2, far_even, far_odd

    field, before = vectors, None
    for step in range(STEPS):
        first, last = step == 0, step == STEPS - 1
        halos = travel(edges)
        extra = () if first else (before,)
        partial, rounded = pl.pallas_call(
            functools.partial(local_kernel, first, rows, cols),
            out_shape=(shape(rows, cols, dtype=jnp.float32), shape(rows, cols)),
            in_specs=[SMEM] + [VMEM] * (2 + len(extra)),
            out_specs=[VMEM] * 2,
            compiler_params=params,
            cost_estimate=cost(220),
            name="local",
        )(place, hamiltonian, field, *extra)
        common = (place, side, hamiltonian, *halos, partial)
        scratch = [pltpu.VMEM((rows + 2, cols + 2, size, trials), jnp.bfloat16)]
        if last:
            return pl.pallas_call(
                functools.partial(rim_kernel, first, last, rows, cols),
                out_shape=shape(rows, cols, dtype=jnp.float32),
                in_specs=[SMEM] * 2 + [VMEM] * 9,
                out_specs=VMEM,
                scratch_shapes=scratch,
                compiler_params=params,
                cost_estimate=cost(68),
                name="rim",
            )(*common)
        total, rounded, *edges = pl.pallas_call(
            functools.partial(rim_kernel, first, last, rows, cols),
            out_shape=(shape(rows, cols, dtype=jnp.float32), shape(rows, cols), *sends),
            in_specs=[SMEM] * 2 + [VMEM] * 10,
            out_specs=[VMEM] * 8,
            scratch_shapes=scratch,
            input_output_aliases={10: 0, 11: 1},
            compiler_params=params,
            cost_estimate=cost(68),
            name="rim",
        )(*common, rounded)
        before, field = (field if first else before_next), rounded
        before_next = total


def solution(mesh):
    placed = (P("gx", "gy", None, None), P("gx", "gy", None, None, None), P("gx", "gy", None))
    return jax.shard_map(
        on_device, mesh=mesh, in_specs=placed, out_specs=P("gx", "gy", None, None), check_vma=False
    )
```

time: 176 us -> 93.4 us (0.53); the launches traced: 174 us -> 93.2 us
  matrix products: 44.4 us -> 0 us
  waiting for transfers between devices: 56.6 us -> 14.5 us
  starting transfers between devices: 26.2 us -> 51.3 us
  local copies, waits for them, and re-layouts: 30.3 us -> 6.17 us
  Pallas kernels: 0 us -> 19.4 us
  other arithmetic: 16 us -> 1.5 us
    dot_general x5 -> x0, matrix products: 44.4 us -> none  [the longest x4 31 us: operate(): jnp.einsum('xyoij,oxyjm->xyim', ordered, stacked, preferred_element_type=...]
    ppermute x16 -> x28, waiting for transfers between devices: 56.6 us -> 14.5 us  [the longest x24 14.5 us: travel(): lax.ppermute(sent, axes, pair)]
    ppermute x16 -> x28, starting transfers between devices: 26.2 us -> 51.3 us  [the longest x24 42.5 us: travel(): lax.ppermute(sent, axes, pair)]
    pallas_call x0 -> x9, Pallas kernels: none -> 19.4 us  [the longest x4 11.2 us: on_device(): pl.pallas_call(functools.partial(local_kernel, first, rows, cols), out_sh...]
    unnamed x14 -> x0, other arithmetic: 13 us -> none
    unnamed x35 -> x8, local copies, waits for them, and re-layouts: 18.7 us -> 5.94 us
    dot_general x1 -> x0, local copies, waits for them, and re-layouts: 8.07 us -> none  [on_device(): jnp.einsum('xyko,xykij->xyoij', onehot, hamiltonian, preferred_element_ty...]
    another operation x3 -> x0, local copies, waits for them, and re-layouts: 2.24 us -> none  [neighbour_stack(): return jnp.stack(views, axis=0)]
  transfers between devices with their start and end apart: 16 -> 28, of which waited for: 15 -> 7; matrix products, arithmetic and copies ran while one was open for 14% -> 2% of each run, Pallas kernels for 0% -> 12%
where the time goes in v1:
time: 93.4 us; the launch traced here: 93.2 us
  starting transfers between devices  51.3 us (55%)
  Pallas kernels  19.4 us (21%)
  waiting for transfers between devices  14.5 us (16%)
  local copies, waits for them, and re-layouts  6.17 us (7%)
  other arithmetic  1.5 us (2%)
    ppermute x24, starting transfers between devices, travel(): lax.ppermute(sent, axes, pair)  42.5 us
    ppermute x24, waiting for transfers between devices, travel(): lax.ppermute(sent, axes, pair)  14.5 us
    pallas_call x4, Pallas kernels, on_device(): pl.pallas_call(functools.partial(local_kernel, first, rows, cols), out_sh...  11.2 us
    ppermute x4, starting transfers between devices, travel(): near2 = lax.ppermute(both, axes, pairs[0])  8.78 us
    pallas_call x4, Pallas kernels, on_device(): pl.pallas_call(functools.partial(rim_kernel, first, last, rows, cols), ou...  7.6 us
    unnamed x8, local copies, waits for them, and re-layouts  5.94 us
  transfers between devices with their start and end apart: 28, of which 7 were waited for; matrix products, arithmetic and copies ran while one was open for 2% of the time, Pallas kernels for 12%

profile of v1, /device:TPU:1, one launch (start us, length us, event | category | flops | bytes accessed | tf_op | source)
XLA Modules:
  0.0 93.2 jit_solution(12134984668745043498)
XLA Ops:
  0.0 0.1 pad_add_fusion.side.refs_1_
  0.1 1.2 %copy-done.2 = bf16[4,8,128,128]{3,2,1,0:T(8,128)(2,1)S(1)} copy-done((bf16[4,8,128,128]{3,2,1,0:T(8,128)(2,1)S(1)}, bf16[4,8,128,128]{3,2,1,0:T(8,128)(2,1)}, u32[]{:S(2)}) %copy-start.2) | copy-done | bytes 1048600
  1.3 0.6 edges.1
  1.9 3.7 %collective-permute-start.2 = (bf16[4,128,128]{2,1,0:T(8,128)(2,1)S(1)}, bf16[4,128,128]{2,1,0:T(8,128)(2,1)S(1)}, u32[]{:S(2)}, u32[]{:S(2)}) collective-permute-start(bf16[4,128,128]{2,1,0:T(8,128)(2,1)S(1)} %get-tuple-element.43), channel_id=1, source_target_pairs={{0,1},{1,0},{2,3},{3,2},{4,5},{5,4},{6,7},{7,6},{8,9},{9,8},{10,11... | collective-permute-start | bytes 393224 | tf_op jit(solution)/shard_map/ppermute | solution.py:152
  5.6 1.7 %collective-permute-start.5 = (bf16[128,128]{1,0:T(8,128)(2,1)S(1)}, bf16[128,128]{1,0:T(8,128)(2,1)S(1)}, u32[]{:S(2)}, u32[]{:S(2)}) collective-permute-start(bf16[128,128]{1,0:T(8,128)(2,1)S(1)} %get-tuple-element.45), channel_id=1, source_target_pairs={{0,249},{1,248},{2,251},{3,250},{4,253},{5,252},{6,255},{7,254},{8... | collective-permute-start | bytes 98312 | tf_op jit(solution)/shard_map/ppermute | solution.py:152
  7.3 3.7 %collective-permute-start.6 = (bf16[128,128]{1,0:T(8,128)(2,1)S(1)}, bf16[128,128]{1,0:T(8,128)(2,1)S(1)}, u32[]{:S(2)}, u32[]{:S(2)}) collective-permute-start(bf16[128,128]{1,0:T(8,128)(2,1)S(1)} %get-tuple-element.46), channel_id=1, source_target_pairs={{0,255},{1,250},{2,249},{3,252},{4,251},{5,254},{6,253},{7,248},{8... | collective-permute-start | bytes 98312 | tf_op jit(solution)/shard_map/ppermute | solution.py:152
  11.0 0.0 collective-permute-start.3
  11.0 5.1 %collective-permute-start = (bf16[8,128,128]{2,1,0:T(8,128)(2,1)S(1)}, bf16[8,128,128]{2,1,0:T(8,128)(2,1)S(1)}, u32[]{:S(2)}, u32[]{:S(2)}) collective-permute-start(bf16[8,128,128]{2,1,0:T(8,128)(2,1)S(1)} %get-tuple-element.41), channel_id=1, source_target_pairs={{0,8},{1,9},{2,10},{3,11},{4,12},{5,13},{6,14},{7,15},{8,0},{9,1},... | collective-permute-start | bytes 786440 | tf_op jit(solution)/shard_map/ppermute | solution.py:152
  16.1 1.4 %select_reduce_fusion = s32[4,8,9]{1,2,0:T(8,128)S(1)} fusion(s32[4,8,9]{2,1,0:T(8,128)} %param.5), kind=kLoop, calls=%fused_computation | loop fusion | flops 7488 | bytes 2304 | tf_op jit(solution)/shard_map/reduce_sum | solution.py:130
  17.5 0.1 copy.10
  17.6 0.1 reshape.4.refs_0_
  17.7 0.1 collective-permute-start.1
  17.8 0.6 collective-permute-done.3.refs_6_
  18.4 4.8 %collective-permute-start.4 = (bf16[2,128,128]{2,1,0:T(8,128)(2,1)S(1)}, bf16[2,128,128]{2,1,0:T(8,128)(2,1)S(1)}, u32[]{:S(2)}, u32[]{:S(2)}) collective-permute-start(bf16[2,128,128]{2,1,0:T(8,128)(2,1)S(1)} %pad_maximum_fusion), channel_id=1, source_target_pairs={{0,8},{1,9},{2,10},{3,11},{4,12},{5,13},{6,14},{7,15},{8,0},{9,1},... | collective-permute-start | bytes 196616 | tf_op jit(solution)/shard_map/ppermute | solution.py:156
  23.3 3.7 %copy-done = bf16[4,8,9,128,128]{4,3,2,1,0:T(8,128)(2,1)S(1)} copy-done((bf16[4,8,9,128,128]{4,3,2,1,0:T(8,128)(2,1)S(1)}, bf16[4,8,9,128,128]{4,3,2,1,0:T(8,128)(2,1)}, u32[]{:S(2)}) %copy-start) | copy-done | bytes 9437208
  27.0 2.6 %local.4 = (f32[4,8,128,128]{3,2,1,0:T(8,128)S(1)}, bf16[4,8,128,128]{3,2,1,0:T(8,128)(2,1)S(1)}) custom-call(s32[288]{0:T(512)S(1)} %reshape.4.refs_0_, bf16[4,8,9,128,128]{4,3,2,1,0:T(8,128)(2,1)S(1)} %copy-done, bf16[4,8,128,128]{3,2,1,0:T(8,128)(2,1)S(1)} %copy-done.3), custom_call_target="tpu_custom_call" | custom-call | flops 922746880 | bytes 7208960 | tf_op jit(solution)/shard_map/local/pallas_call | solution.py:164
  29.6 0.0 collective-permute-done.5.refs_8_
  29.6 1.0 %copy-done.1 = bf16[4,8,9,128,128]{4,3,2,1,0:T(8,128)(2,1)S(1)} copy-done((bf16[4,8,9,128,128]{4,3,2,1,0:T(8,128)(2,1)S(1)}, bf16[4,8,9,128,128]{4,3,2,1,0:T(8,128)(2,1)}, u32[]{:S(2)}) %copy-start.1) | copy-done | bytes 9437208
  30.6 1.6 %rim.4 = (f32[4,8,128,128]{3,2,1,0:T(8,128)S(1)}, bf16[4,8,128,128]{3,2,1,0:T(8,128)(2,1)S(1)}, bf16[8,128,128]{2,1,0:T(8,128)(2,1)S(1)}, bf16[8,128,128]{2,1,0:...) custom-call(s32[288]{0:T(512)S(1)} %reshape.4.refs_0_, ...), custom_call_target="tpu_custom_call", output_to_operand_aliasing={{0}: (10, {}), {1}: (11, {})} | custom-call | flops 285212672 | bytes 2228224 | tf_op jit(solution)/shard_map/rim/pallas_call | solution.py:186
  32.2 2.1 %collective-permute-start.9 = (bf16[4,128,128]{2,1,0:T(8,128)(2,1)S(1)}, bf16[4,128,128]{2,1,0:T(8,128)(2,1)S(1)}, u32[]{:S(2)}, u32[]{:S(2)}) collective-permute-start(bf16[4,128,128]{2,1,0:T(8,128)(2,1)S(1)} %get-tuple-element.51), channel_id=1, source_target_pairs={{0,1},{1,0},{2,3},{3,2},{4,5},{5,4},{6,7},{7,6},{8,9},{9,8},{10,11... | collective-permute-start | bytes 393224 | tf_op jit(solution)/shard_map/ppermute | solution.py:152
  34.4 2.9 %collective-permute-start.10 = (bf16[4,128,128]{2,1,0:T(8,128)(2,1)S(1)}, bf16[4,128,128]{2,1,0:T(8,128)(2,1)S(1)}, u32[]{:S(2)}, u32[]{:S(2)}) collective-permute-start(bf16[4,128,128]{2,1,0:T(8,128)(2,1)S(1)} %get-tuple-element.52), channel_id=1, source_target_pairs={{0,7},{1,2},{2,1},{3,4},{4,3},{5,6},{6,5},{7,0},{8,15},{9,10},{10,... | collective-permute-start | bytes 393224 | tf_op jit(solution)/shard_map/ppermute | solution.py:152
  37.3 2.9 %collective-permute-start.13 = (bf16[128,128]{1,0:T(8,128)(2,1)S(1)}, bf16[128,128]{1,0:T(8,128)(2,1)S(1)}, u32[]{:S(2)}, u32[]{:S(2)}) collective-permute-start(bf16[128,128]{1,0:T(8,128)(2,1)S(1)} %get-tuple-element.54), channel_id=1, source_target_pairs={{0,255},{1,250},{2,249},{3,252},{4,251},{5,254},{6,253},{7,248},{8... | collective-permute-start | bytes 98312 | tf_op jit(solution)/shard_map/ppermute | solution.py:152
  40.2 2.6 %collective-permute-start.7 = (bf16[8,128,128]{2,1,0:T(8,128)(2,1)S(1)}, bf16[8,128,128]{2,1,0:T(8,128)(2,1)S(1)}, u32[]{:S(2)}, u32[]{:S(2)}) collective-permute-start(bf16[8,128,128]{2,1,0:T(8,128)(2,1)S(1)} %get-tuple-element.49), channel_id=1, source_target_pairs={{0,8},{1,9},{2,10},{3,11},{4,12},{5,13},{6,14},{7,15},{8,0},{9,1},... | collective-permute-start | bytes 786440 | tf_op jit(solution)/shard_map/ppermute | solution.py:152
  42.7 1.1 %collective-permute-done.10.refs_6_ = bf16[4,128,128]{2,1,0:T(8,128)(2,1)S(1)} collective-permute-done((bf16[4,128,128]{2,1,0:T(8,128)(2,1)S(1)}, bf16[4,128,128]{2,1,0:T(8,128)(2,1)S(1)}, u32[]{:S(2)}, u32[]{:S(2)}) %collective-permute-start.10) | collective-permute-done | bytes 131104 | tf_op jit(solution)/shard_map/ppermute | solution.py:152
  43.9 1.3 %collective-permute-start.11 = (bf16[2,128,128]{2,1,0:T(8,128)(2,1)S(1)}, bf16[2,128,128]{2,1,0:T(8,128)(2,1)S(1)}, u32[]{:S(2)}, u32[]{:S(2)}) collective-permute-start(bf16[2,128,128]{2,1,0:T(8,128)(2,1)S(1)} %pad_maximum_fusion.1), channel_id=1, source_target_pairs={{0,8},{1,9},{2,10},{3,11},{4,12},{5,13},{6,14},{7,15},{8,0},{9,1},... | collective-permute-start | bytes 196616 | tf_op jit(solution)/shard_map/ppermute | solution.py:156
  45.2 2.6 %local.5 = (f32[4,8,128,128]{3,2,1,0:T(8,128)S(1)}, bf16[4,8,128,128]{3,2,1,0:T(8,128)(2,1)S(1)}) custom-call(s32[288]{0:T(512)S(1)} %reshape.4.refs_0_, bf16[4,8,9,128,128]{4,3,2,1,0:T(8,128)(2,1)S(1)} %copy-done.1, bf16[4,8,128,128]{3,2,1,0:T(8,128)(2,1)S(1)} %get-tuple-element.55.refs_2_, bf16[4,8,128,128]{3,2,1,0:T(8,128)(2,1)S(1)} %copy-done.3), custom_call_target="tpu_custom_call" | custom-call | flops 922746880 | bytes 7208960 | tf_op jit(solution)/shard_map/local/pallas_call | solution.py:164
  47.8 4.3 %collective-permute-done.8.refs_4_ = bf16[8,128,128]{2,1,0:T(8,128)(2,1)S(1)} collective-permute-done((bf16[8,128,128]{2,1,0:T(8,128)(2,1)S(1)}, bf16[8,128,128]{2,1,0:T(8,128)(2,1)S(1)}, u32[]{:S(2)}, u32[]{:S(2)}) %collective-permute-start.8) | collective-permute-done | bytes 262176 | tf_op jit(solution)/shard_map/ppermute | solution.py:152
  52.1 1.6 %rim.5 = (f32[4,8,128,128]{3,2,1,0:T(8,128)S(1)}, bf16[4,8,128,128]{3,2,1,0:T(8,128)(2,1)S(1)}, bf16[8,128,128]{2,1,0:T(8,128)(2,1)S(1)}, bf16[8,128,128]{2,1,0:...) custom-call(s32[288]{0:T(512)S(1)} %reshape.4.refs_0_, ...), custom_call_target="tpu_custom_call", output_to_operand_aliasing={{0}: (10, {}), {1}: (11, {})} | custom-call | flops 285212672 | bytes 2228224 | tf_op jit(solution)/shard_map/rim/pallas_call | solution.py:186
  53.8 0.1 collective-permute-start.16
  53.9 2.7 %collective-permute-start.17 = (bf16[4,128,128]{2,1,0:T(8,128)(2,1)S(1)}, bf16[4,128,128]{2,1,0:T(8,128)(2,1)S(1)}, u32[]{:S(2)}, u32[]{:S(2)}) collective-permute-start(bf16[4,128,128]{2,1,0:T(8,128)(2,1)S(1)} %get-tuple-element.61), channel_id=1, source_target_pairs={{0,7},{1,2},{2,1},{3,4},{4,3},{5,6},{6,5},{7,0},{8,15},{9,10},{10,... | collective-permute-start | bytes 393224 | tf_op jit(solution)/shard_map/ppermute | solution.py:152
  56.6 0.9 collective-permute-start.19
  57.4 3.1 %collective-permute-start.20 = (bf16[128,128]{1,0:T(8,128)(2,1)S(1)}, bf16[128,128]{1,0:T(8,128)(2,1)S(1)}, u32[]{:S(2)}, u32[]{:S(2)}) collective-permute-start(bf16[128,128]{1,0:T(8,128)(2,1)S(1)} %get-tuple-element.63), channel_id=1, source_target_pairs={{0,255},{1,250},{2,249},{3,252},{4,251},{5,254},{6,253},{7,248},{8... | collective-permute-start | bytes 98312 | tf_op jit(solution)/shard_map/ppermute | solution.py:152
  60.5 1.6 %collective-permute-start.14 = (bf16[8,128,128]{2,1,0:T(8,128)(2,1)S(1)}, bf16[8,128,128]{2,1,0:T(8,128)(2,1)S(1)}, u32[]{:S(2)}, u32[]{:S(2)}) collective-permute-start(bf16[8,128,128]{2,1,0:T(8,128)(2,1)S(1)} %get-tuple-element.58), channel_id=1, source_target_pairs={{0,8},{1,9},{2,10},{3,11},{4,12},{5,13},{6,14},{7,15},{8,0},{9,1},... | collective-permute-start | bytes 786440 | tf_op jit(solution)/shard_map/ppermute | solution.py:152
  62.1 0.3 collective-permute-done.17.refs_6_
  62.4 2.0 %collective-permute-start.18 = (bf16[2,128,128]{2,1,0:T(8,128)(2,1)S(1)}, bf16[2,128,128]{2,1,0:T(8,128)(2,1)S(1)}, u32[]{:S(2)}, u32[]{:S(2)}) collective-permute-start(bf16[2,128,128]{2,1,0:T(8,128)(2,1)S(1)} %pad_maximum_fusion.2), channel_id=1, source_target_pairs={{0,8},{1,9},{2,10},{3,11},{4,12},{5,13},{6,14},{7,15},{8,0},{9,1},... | collective-permute-start | bytes 196616 | tf_op jit(solution)/shard_map/ppermute | solution.py:156
  64.4 2.6 %local.6 = (f32[4,8,128,128]{3,2,1,0:T(8,128)S(1)}, bf16[4,8,128,128]{3,2,1,0:T(8,128)(2,1)S(1)}) custom-call(s32[288]{0:T(512)S(1)} %reshape.4.refs_0_, bf16[4,8,9,128,128]{4,3,2,1,0:T(8,128)(2,1)S(1)} %copy-done.1, bf16[4,8,128,128]{3,2,1,0:T(8,128)(2,1)S(1)} %get-tuple-element.64.refs_2_, f32[4,8,128,128]{3,2,1,0:T(8,128)S(1)} %get-tuple-element.65.refs_3_), custom_call_target="tpu_custom_call" | custom-call | flops 922746880 | bytes 7208960 | tf_op jit(solution)/shard_map/local/pallas_call | solution.py:164
  67.0 3.7 %collective-permute-done.15.refs_4_ = bf16[8,128,128]{2,1,0:T(8,128)(2,1)S(1)} collective-permute-done((bf16[8,128,128]{2,1,0:T(8,128)(2,1)S(1)}, bf16[8,128,128]{2,1,0:T(8,128)(2,1)S(1)}, u32[]{:S(2)}, u32[]{:S(2)}) %collective-permute-start.15) | collective-permute-done | bytes 262176 | tf_op jit(solution)/shard_map/ppermute | solution.py:152
  70.7 1.6 %rim.6 = (f32[4,8,128,128]{3,2,1,0:T(8,128)S(1)}, bf16[4,8,128,128]{3,2,1,0:T(8,128)(2,1)S(1)}, bf16[8,128,128]{2,1,0:T(8,128)(2,1)S(1)}, bf16[8,128,128]{2,1,0:...) custom-call(s32[288]{0:T(512)S(1)} %reshape.4.refs_0_, ...), custom_call_target="tpu_custom_call", output_to_operand_aliasing={{0}: (10, {}), {1}: (11, {})} | custom-call | flops 285212672 | bytes 2228224 | tf_op jit(solution)/shard_map/rim/pallas_call | solution.py:186
  72.4 1.4 %collective-permute-start.23 = (bf16[4,128,128]{2,1,0:T(8,128)(2,1)S(1)}, bf16[4,128,128]{2,1,0:T(8,128)(2,1)S(1)}, u32[]{:S(2)}, u32[]{:S(2)}) collective-permute-start(bf16[4,128,128]{2,1,0:T(8,128)(2,1)S(1)} %get-tuple-element.70), channel_id=1, source_target_pairs={{0,1},{1,0},{2,3},{3,2},{4,5},{5,4},{6,7},{7,6},{8,9},{9,8},{10,11... | collective-permute-start | bytes 393224 | tf_op jit(solution)/shard_map/ppermute | solution.py:152
  73.8 3.0 %collective-permute-start.24 = (bf16[4,128,128]{2,1,0:T(8,128)(2,1)S(1)}, bf16[4,128,128]{2,1,0:T(8,128)(2,1)S(1)}, u32[]{:S(2)}, u32[]{:S(2)}) collective-permute-start(bf16[4,128,128]{2,1,0:T(8,128)(2,1)S(1)} %get-tuple-element.71), channel_id=1, source_target_pairs={{0,7},{1,2},{2,1},{3,4},{4,3},{5,6},{6,5},{7,0},{8,15},{9,10},{10,... | collective-permute-start | bytes 393224 | tf_op jit(solution)/shard_map/ppermute | solution.py:152
  76.8 3.0 %collective-permute-start.27 = (bf16[128,128]{1,0:T(8,128)(2,1)S(1)}, bf16[128,128]{1,0:T(8,128)(2,1)S(1)}, u32[]{:S(2)}, u32[]{:S(2)}) collective-permute-start(bf16[128,128]{1,0:T(8,128)(2,1)S(1)} %get-tuple-element.73), channel_id=1, source_target_pairs={{0,255},{1,250},{2,249},{3,252},{4,251},{5,254},{6,253},{7,248},{8... | collective-permute-start | bytes 98312 | tf_op jit(solution)/shard_map/ppermute | solution.py:152
  79.8 2.1 %collective-permute-start.21 = (bf16[8,128,128]{2,1,0:T(8,128)(2,1)S(1)}, bf16[8,128,128]{2,1,0:T(8,128)(2,1)S(1)}, u32[]{:S(2)}, u32[]{:S(2)}) collective-permute-start(bf16[8,128,128]{2,1,0:T(8,128)(2,1)S(1)} %get-tuple-element.68), channel_id=1, source_target_pairs={{0,8},{1,9},{2,10},{3,11},{4,12},{5,13},{6,14},{7,15},{8,0},{9,1},... | collective-permute-start | bytes 786440 | tf_op jit(solution)/shard_map/ppermute | solution.py:152
  81.8 0.0 collective-permute-start.22
  81.8 1.8 %collective-permute-done.24.refs_6_ = bf16[4,128,128]{2,1,0:T(8,128)(2,1)S(1)} collective-permute-done((bf16[4,128,128]{2,1,0:T(8,128)(2,1)S(1)}, bf16[4,128,128]{2,1,0:T(8,128)(2,1)S(1)}, u32[]{:S(2)}, u32[]{:S(2)}) %collective-permute-start.24) | collective-permute-done | bytes 131104 | tf_op jit(solution)/shard_map/ppermute | solution.py:152
  83.7 0.6 collective-permute-start.25
  84.3 3.4 %local.7 = (f32[4,8,128,128]{3,2,1,0:T(8,128)S(1)}, bf16[4,8,128,128]{3,2,1,0:T(8,128)(2,1)}) custom-call(s32[288]{0:T(512)S(1)} %reshape.4.refs_0_, bf16[4,8,9,128,128]{4,3,2,1,0:T(8,128)(2,1)S(1)} %copy-done.1, bf16[4,8,128,128]{3,2,1,0:T(8,128)(2,1)S(1)} %get-tuple-element.74.refs_2_, f32[4,8,128,128]{3,2,1,0:T(8,128)S(1)} %get-tuple-element.75.refs_3_), custom_call_target="tpu_custom_call" | custom-call | flops 922746880 | bytes 7208960 | tf_op jit(solution)/shard_map/local/pallas_call | solution.py:164
  87.7 2.7 %collective-permute-done.22.refs_4_ = bf16[8,128,128]{2,1,0:T(8,128)(2,1)S(1)} collective-permute-done((bf16[8,128,128]{2,1,0:T(8,128)(2,1)S(1)}, bf16[8,128,128]{2,1,0:T(8,128)(2,1)S(1)}, u32[]{:S(2)}, u32[]{:S(2)}) %collective-permute-start.22) | collective-permute-done | bytes 262176 | tf_op jit(solution)/shard_map/ppermute | solution.py:152
  90.4 2.7 %rim.7 = f32[4,8,128,128]{3,2,1,0:T(8,128)} custom-call(s32[288]{0:T(512)S(1)} %reshape.4.refs_0_, s32[2]{0:T(128)S(1)} %pad_add_fusion.side.refs_1_, bf16[4,8,9,128,128]{4,3,2,1,0:T(8,128)(2,1)S(1)} %copy-done.1, bf16[8,128,128]{2,1,0:T(8,128)(2,1)S(1)} %collective-permute-done.21.refs_3_, bf16[8,128,128]{2,1,0:T(8,128)(2,1)S(1)} %collective-permute-done.22.refs_4_, ...), custom_call_target="tpu_custom_call" | custom-call | flops 285212672 | bytes 2228224 | tf_op jit(solution)/shard_map/rim/pallas_call | solution.py:176
  (41 shorter events, 0.1 us)
Async XLA Ops:
  0.1 1.2 %copy-start.2 = (bf16[4,8,128,128]{3,2,1,0:T(8,128)(2,1)S(1)}, bf16[4,8,128,128]{3,2,1,0:T(8,128)(2,1)}, u32[]{:S(2)}) copy-start(bf16[4,8,128,128]{3,2,1,0:T(8,128)(2,1)} %refs_3_.1) | copy-start | bytes 3145732
  1.3 22.0 %copy-start.3 = (bf16[4,8,128,128]{3,2,1,0:T(8,128)(2,1)S(1)}, bf16[4,8,128,128]{3,2,1,0:T(8,128)(2,1)}, u32[]{:S(2)}) copy-start(bf16[4,8,128,128]{3,2,1,0:T(8,128)(2,1)} %refs_3_.1) | copy-start | bytes 3145732
  1.9 15.8 %collective-permute-start.2 = (bf16[4,128,128]{2,1,0:T(8,128)(2,1)S(1)}, bf16[4,128,128]{2,1,0:T(8,128)(2,1)S(1)}, u32[]{:S(2)}, u32[]{:S(2)}) collective-permute-start(bf16[4,128,128]{2,1,0:T(8,128)(2,1)S(1)} %get-tuple-element.43), channel_id=1, source_target_pairs={{0,1},{1,0},{2,3},{3,2},{4,5},{5,4},{6,7},{7,6},{8,9},{9,8},{10,11... | collective-permute-start | bytes 393224 | tf_op jit(solution)/shard_map/ppermute | solution.py:152
  5.6 24.0 %collective-permute-start.5 = (bf16[128,128]{1,0:T(8,128)(2,1)S(1)}, bf16[128,128]{1,0:T(8,128)(2,1)S(1)}, u32[]{:S(2)}, u32[]{:S(2)}) collective-permute-start(bf16[128,128]{1,0:T(8,128)(2,1)S(1)} %get-tuple-element.45), channel_id=1, source_target_pairs={{0,249},{1,248},{2,251},{3,250},{4,253},{5,252},{6,255},{7,254},{8... | collective-permute-start | bytes 98312 | tf_op jit(solution)/shard_map/ppermute | solution.py:152
  7.3 22.3 %collective-permute-start.6 = (bf16[128,128]{1,0:T(8,128)(2,1)S(1)}, bf16[128,128]{1,0:T(8,128)(2,1)S(1)}, u32[]{:S(2)}, u32[]{:S(2)}) collective-permute-start(bf16[128,128]{1,0:T(8,128)(2,1)S(1)} %get-tuple-element.46), channel_id=1, source_target_pairs={{0,255},{1,250},{2,249},{3,252},{4,251},{5,254},{6,253},{7,248},{8... | collective-permute-start | bytes 98312 | tf_op jit(solution)/shard_map/ppermute | solution.py:152
  11.0 7.4 %collective-permute-start.3 = (bf16[4,128,128]{2,1,0:T(8,128)(2,1)S(1)}, bf16[4,128,128]{2,1,0:T(8,128)(2,1)S(1)}, u32[]{:S(2)}, u32[]{:S(2)}) collective-permute-start(bf16[4,128,128]{2,1,0:T(8,128)(2,1)S(1)} %get-tuple-element.44), channel_id=1, source_target_pairs={{0,7},{1,2},{2,1},{3,4},{4,3},{5,6},{6,5},{7,0},{8,15},{9,10},{10,... | collective-permute-start | bytes 393224 | tf_op jit(solution)/shard_map/ppermute | solution.py:152
  11.0 18.6 %collective-permute-start = (bf16[8,128,128]{2,1,0:T(8,128)(2,1)S(1)}, bf16[8,128,128]{2,1,0:T(8,128)(2,1)S(1)}, u32[]{:S(2)}, u32[]{:S(2)}) collective-permute-start(bf16[8,128,128]{2,1,0:T(8,128)(2,1)S(1)} %get-tuple-element.41), channel_id=1, source_target_pairs={{0,8},{1,9},{2,10},{3,11},{4,12},{5,13},{6,14},{7,15},{8,0},{9,1},... | collective-permute-start | bytes 786440 | tf_op jit(solution)/shard_map/ppermute | solution.py:152
  17.7 11.9 %collective-permute-start.1 = (bf16[8,128,128]{2,1,0:T(8,128)(2,1)S(1)}, bf16[8,128,128]{2,1,0:T(8,128)(2,1)S(1)}, u32[]{:S(2)}, u32[]{:S(2)}) collective-permute-start(bf16[8,128,128]{2,1,0:T(8,128)(2,1)S(1)} %get-tuple-element.42), channel_id=1, source_target_pairs={{0,248},{1,249},{2,250},{3,251},{4,252},{5,253},{6,254},{7,255},{8... | collective-permute-start | bytes 786440 | tf_op jit(solution)/shard_map/ppermute | solution.py:152
  18.4 11.1 %collective-permute-start.4 = (bf16[2,128,128]{2,1,0:T(8,128)(2,1)S(1)}, bf16[2,128,128]{2,1,0:T(8,128)(2,1)S(1)}, u32[]{:S(2)}, u32[]{:S(2)}) collective-permute-start(bf16[2,128,128]{2,1,0:T(8,128)(2,1)S(1)} %pad_maximum_fusion), channel_id=1, source_target_pairs={{0,8},{1,9},{2,10},{3,11},{4,12},{5,13},{6,14},{7,15},{8,0},{9,1},... | collective-permute-start | bytes 196616 | tf_op jit(solution)/shard_map/ppermute | solution.py:156
  23.3 3.7 %copy-start = (bf16[4,8,9,128,128]{4,3,2,1,0:T(8,128)(2,1)S(1)}, bf16[4,8,9,128,128]{4,3,2,1,0:T(8,128)(2,1)}, u32[]{:S(2)}) copy-start(bf16[4,8,9,128,128]{4,3,2,1,0:T(8,128)(2,1)} %refs_2_.9) | copy-start | bytes 28311556
  27.0 3.7 %copy-start.1 = (bf16[4,8,9,128,128]{4,3,2,1,0:T(8,128)(2,1)S(1)}, bf16[4,8,9,128,128]{4,3,2,1,0:T(8,128)(2,1)}, u32[]{:S(2)}) copy-start(bf16[4,8,9,128,128]{4,3,2,1,0:T(8,128)(2,1)} %refs_2_.9) | copy-start | bytes 28311556
  32.2 10.5 %collective-permute-start.9 = (bf16[4,128,128]{2,1,0:T(8,128)(2,1)S(1)}, bf16[4,128,128]{2,1,0:T(8,128)(2,1)S(1)}, u32[]{:S(2)}, u32[]{:S(2)}) collective-permute-start(bf16[4,128,128]{2,1,0:T(8,128)(2,1)S(1)} %get-tuple-element.51), channel_id=1, source_target_pairs={{0,1},{1,0},{2,3},{3,2},{4,5},{5,4},{6,7},{7,6},{8,9},{9,8},{10,11... | collective-permute-start | bytes 393224 | tf_op jit(solution)/shard_map/ppermute | solution.py:152
  34.4 9.5 %collective-permute-start.10 = (bf16[4,128,128]{2,1,0:T(8,128)(2,1)S(1)}, bf16[4,128,128]{2,1,0:T(8,128)(2,1)S(1)}, u32[]{:S(2)}, u32[]{:S(2)}) collective-permute-start(bf16[4,128,128]{2,1,0:T(8,128)(2,1)S(1)} %get-tuple-element.52), channel_id=1, source_target_pairs={{0,7},{1,2},{2,1},{3,4},{4,3},{5,6},{6,5},{7,0},{8,15},{9,10},{10,... | collective-permute-start | bytes 393224 | tf_op jit(solution)/shard_map/ppermute | solution.py:152
  37.3 10.5 %collective-permute-start.12 = (bf16[128,128]{1,0:T(8,128)(2,1)S(1)}, bf16[128,128]{1,0:T(8,128)(2,1)S(1)}, u32[]{:S(2)}, u32[]{:S(2)}) collective-permute-start(bf16[128,128]{1,0:T(8,128)(2,1)S(1)} %get-tuple-element.53), channel_id=1, source_target_pairs={{0,249},{1,248},{2,251},{3,250},{4,253},{5,252},{6,255},{7,254},{8... | collective-permute-start | bytes 98312 | tf_op jit(solution)/shard_map/ppermute | solution.py:152
  37.3 10.5 %collective-permute-start.13 = (bf16[128,128]{1,0:T(8,128)(2,1)S(1)}, bf16[128,128]{1,0:T(8,128)(2,1)S(1)}, u32[]{:S(2)}, u32[]{:S(2)}) collective-permute-start(bf16[128,128]{1,0:T(8,128)(2,1)S(1)} %get-tuple-element.54), channel_id=1, source_target_pairs={{0,255},{1,250},{2,249},{3,252},{4,251},{5,254},{6,253},{7,248},{8... | collective-permute-start | bytes 98312 | tf_op jit(solution)/shard_map/ppermute | solution.py:152
  40.2 7.7 %collective-permute-start.7 = (bf16[8,128,128]{2,1,0:T(8,128)(2,1)S(1)}, bf16[8,128,128]{2,1,0:T(8,128)(2,1)S(1)}, u32[]{:S(2)}, u32[]{:S(2)}) collective-permute-start(bf16[8,128,128]{2,1,0:T(8,128)(2,1)S(1)} %get-tuple-element.49), channel_id=1, source_target_pairs={{0,8},{1,9},{2,10},{3,11},{4,12},{5,13},{6,14},{7,15},{8,0},{9,1},... | collective-permute-start | bytes 786440 | tf_op jit(solution)/shard_map/ppermute | solution.py:152
  42.7 9.4 %collective-permute-start.8 = (bf16[8,128,128]{2,1,0:T(8,128)(2,1)S(1)}, bf16[8,128,128]{2,1,0:T(8,128)(2,1)S(1)}, u32[]{:S(2)}, u32[]{:S(2)}) collective-permute-start(bf16[8,128,128]{2,1,0:T(8,128)(2,1)S(1)} %get-tuple-element.50), channel_id=1, source_target_pairs={{0,248},{1,249},{2,250},{3,251},{4,252},{5,253},{6,254},{7,255},{8... | collective-permute-start | bytes 786440 | tf_op jit(solution)/shard_map/ppermute | solution.py:152
  43.9 3.9 %collective-permute-start.11 = (bf16[2,128,128]{2,1,0:T(8,128)(2,1)S(1)}, bf16[2,128,128]{2,1,0:T(8,128)(2,1)S(1)}, u32[]{:S(2)}, u32[]{:S(2)}) collective-permute-start(bf16[2,128,128]{2,1,0:T(8,128)(2,1)S(1)} %pad_maximum_fusion.1), channel_id=1, source_target_pairs={{0,8},{1,9},{2,10},{3,11},{4,12},{5,13},{6,14},{7,15},{8,0},{9,1},... | collective-permute-start | bytes 196616 | tf_op jit(solution)/shard_map/ppermute | solution.py:156
  53.8 8.3 %collective-permute-start.16 = (bf16[4,128,128]{2,1,0:T(8,128)(2,1)S(1)}, bf16[4,128,128]{2,1,0:T(8,128)(2,1)S(1)}, u32[]{:S(2)}, u32[]{:S(2)}) collective-permute-start(bf16[4,128,128]{2,1,0:T(8,128)(2,1)S(1)} %get-tuple-element.60), channel_id=1, source_target_pairs={{0,1},{1,0},{2,3},{3,2},{4,5},{5,4},{6,7},{7,6},{8,9},{9,8},{10,11... | collective-permute-start | bytes 393224 | tf_op jit(solution)/shard_map/ppermute | solution.py:152
  53.9 8.5 %collective-permute-start.17 = (bf16[4,128,128]{2,1,0:T(8,128)(2,1)S(1)}, bf16[4,128,128]{2,1,0:T(8,128)(2,1)S(1)}, u32[]{:S(2)}, u32[]{:S(2)}) collective-permute-start(bf16[4,128,128]{2,1,0:T(8,128)(2,1)S(1)} %get-tuple-element.61), channel_id=1, source_target_pairs={{0,7},{1,2},{2,1},{3,4},{4,3},{5,6},{6,5},{7,0},{8,15},{9,10},{10,... | collective-permute-start | bytes 393224 | tf_op jit(solution)/shard_map/ppermute | solution.py:152
  56.6 10.4 %collective-permute-start.19 = (bf16[128,128]{1,0:T(8,128)(2,1)S(1)}, bf16[128,128]{1,0:T(8,128)(2,1)S(1)}, u32[]{:S(2)}, u32[]{:S(2)}) collective-permute-start(bf16[128,128]{1,0:T(8,128)(2,1)S(1)} %get-tuple-element.62), channel_id=1, source_target_pairs={{0,249},{1,248},{2,251},{3,250},{4,253},{5,252},{6,255},{7,254},{8... | collective-permute-start | bytes 98312 | tf_op jit(solution)/shard_map/ppermute | solution.py:152
  57.4 9.6 %collective-permute-start.20 = (bf16[128,128]{1,0:T(8,128)(2,1)S(1)}, bf16[128,128]{1,0:T(8,128)(2,1)S(1)}, u32[]{:S(2)}, u32[]{:S(2)}) collective-permute-start(bf16[128,128]{1,0:T(8,128)(2,1)S(1)} %get-tuple-element.63), channel_id=1, source_target_pairs={{0,255},{1,250},{2,249},{3,252},{4,251},{5,254},{6,253},{7,248},{8... | collective-permute-start | bytes 98312 | tf_op jit(solution)/shard_map/ppermute | solution.py:152
  60.5 6.5 %collective-permute-start.14 = (bf16[8,128,128]{2,1,0:T(8,128)(2,1)S(1)}, bf16[8,128,128]{2,1,0:T(8,128)(2,1)S(1)}, u32[]{:S(2)}, u32[]{:S(2)}) collective-permute-start(bf16[8,128,128]{2,1,0:T(8,128)(2,1)S(1)} %get-tuple-element.58), channel_id=1, source_target_pairs={{0,8},{1,9},{2,10},{3,11},{4,12},{5,13},{6,14},{7,15},{8,0},{9,1},... | collective-permute-start | bytes 786440 | tf_op jit(solution)/shard_map/ppermute | solution.py:152
  62.1 8.6 %collective-permute-start.15 = (bf16[8,128,128]{2,1,0:T(8,128)(2,1)S(1)}, bf16[8,128,128]{2,1,0:T(8,128)(2,1)S(1)}, u32[]{:S(2)}, u32[]{:S(2)}) collective-permute-start(bf16[8,128,128]{2,1,0:T(8,128)(2,1)S(1)} %get-tuple-element.59), channel_id=1, source_target_pairs={{0,248},{1,249},{2,250},{3,251},{4,252},{5,253},{6,254},{7,255},{8... | collective-permute-start | bytes 786440 | tf_op jit(solution)/shard_map/ppermute | solution.py:152
  62.4 4.6 %collective-permute-start.18 = (bf16[2,128,128]{2,1,0:T(8,128)(2,1)S(1)}, bf16[2,128,128]{2,1,0:T(8,128)(2,1)S(1)}, u32[]{:S(2)}, u32[]{:S(2)}) collective-permute-start(bf16[2,128,128]{2,1,0:T(8,128)(2,1)S(1)} %pad_maximum_fusion.2), channel_id=1, source_target_pairs={{0,8},{1,9},{2,10},{3,11},{4,12},{5,13},{6,14},{7,15},{8,0},{9,1},... | collective-permute-start | bytes 196616 | tf_op jit(solution)/shard_map/ppermute | solution.py:156
  72.4 9.5 %collective-permute-start.23 = (bf16[4,128,128]{2,1,0:T(8,128)(2,1)S(1)}, bf16[4,128,128]{2,1,0:T(8,128)(2,1)S(1)}, u32[]{:S(2)}, u32[]{:S(2)}) collective-permute-start(bf16[4,128,128]{2,1,0:T(8,128)(2,1)S(1)} %get-tuple-element.70), channel_id=1, source_target_pairs={{0,1},{1,0},{2,3},{3,2},{4,5},{5,4},{6,7},{7,6},{8,9},{9,8},{10,11... | collective-permute-start | bytes 393224 | tf_op jit(solution)/shard_map/ppermute | solution.py:152
  73.8 9.9 %collective-permute-start.24 = (bf16[4,128,128]{2,1,0:T(8,128)(2,1)S(1)}, bf16[4,128,128]{2,1,0:T(8,128)(2,1)S(1)}, u32[]{:S(2)}, u32[]{:S(2)}) collective-permute-start(bf16[4,128,128]{2,1,0:T(8,128)(2,1)S(1)} %get-tuple-element.71), channel_id=1, source_target_pairs={{0,7},{1,2},{2,1},{3,4},{4,3},{5,6},{6,5},{7,0},{8,15},{9,10},{10,... | collective-permute-start | bytes 393224 | tf_op jit(solution)/shard_map/ppermute | solution.py:152
  76.8 10.9 %collective-permute-start.26 = (bf16[128,128]{1,0:T(8,128)(2,1)S(1)}, bf16[128,128]{1,0:T(8,128)(2,1)S(1)}, u32[]{:S(2)}, u32[]{:S(2)}) collective-permute-start(bf16[128,128]{1,0:T(8,128)(2,1)S(1)} %get-tuple-element.72), channel_id=1, source_target_pairs={{0,249},{1,248},{2,251},{3,250},{4,253},{5,252},{6,255},{7,254},{8... | collective-permute-start | bytes 98312 | tf_op jit(solution)/shard_map/ppermute | solution.py:152
  76.8 10.9 %collective-permute-start.27 = (bf16[128,128]{1,0:T(8,128)(2,1)S(1)}, bf16[128,128]{1,0:T(8,128)(2,1)S(1)}, u32[]{:S(2)}, u32[]{:S(2)}) collective-permute-start(bf16[128,128]{1,0:T(8,128)(2,1)S(1)} %get-tuple-element.73), channel_id=1, source_target_pairs={{0,255},{1,250},{2,249},{3,252},{4,251},{5,254},{6,253},{7,248},{8... | collective-permute-start | bytes 98312 | tf_op jit(solution)/shard_map/ppermute | solution.py:152
  79.8 8.0 %collective-permute-start.21 = (bf16[8,128,128]{2,1,0:T(8,128)(2,1)S(1)}, bf16[8,128,128]{2,1,0:T(8,128)(2,1)S(1)}, u32[]{:S(2)}, u32[]{:S(2)}) collective-permute-start(bf16[8,128,128]{2,1,0:T(8,128)(2,1)S(1)} %get-tuple-element.68), channel_id=1, source_target_pairs={{0,8},{1,9},{2,10},{3,11},{4,12},{5,13},{6,14},{7,15},{8,0},{9,1},... | collective-permute-start | bytes 786440 | tf_op jit(solution)/shard_map/ppermute | solution.py:152
  81.8 8.6 %collective-permute-start.22 = (bf16[8,128,128]{2,1,0:T(8,128)(2,1)S(1)}, bf16[8,128,128]{2,1,0:T(8,128)(2,1)S(1)}, u32[]{:S(2)}, u32[]{:S(2)}) collective-permute-start(bf16[8,128,128]{2,1,0:T(8,128)(2,1)S(1)} %get-tuple-element.69), channel_id=1, source_target_pairs={{0,248},{1,249},{2,250},{3,251},{4,252},{5,253},{6,254},{7,255},{8... | collective-permute-start | bytes 786440 | tf_op jit(solution)/shard_map/ppermute | solution.py:152
  83.7 4.1 %collective-permute-start.25 = (bf16[2,128,128]{2,1,0:T(8,128)(2,1)S(1)}, bf16[2,128,128]{2,1,0:T(8,128)(2,1)S(1)}, u32[]{:S(2)}, u32[]{:S(2)}) collective-permute-start(bf16[2,128,128]{2,1,0:T(8,128)(2,1)S(1)} %pad_maximum_fusion.3), channel_id=1, source_target_pairs={{0,8},{1,9},{2,10},{3,11},{4,12},{5,13},{6,14},{7,15},{8,0},{9,1},... | collective-permute-start | bytes 196616 | tf_op jit(solution)/shard_map/ppermute | solution.py:156

commit v2 on v0

v2 whole, which is shorter than its diff:
```python
import functools

import jax
import jax.numpy as jnp
from jax import lax
from jax.experimental import pallas as pl
from jax.experimental.pallas import tpu as pltpu
from jax.sharding import PartitionSpec as P

STEPS = 4
NBR = 9
VMEM = pl.BlockSpec(memory_space=pltpu.VMEM)
SMEM = pl.BlockSpec(memory_space=pltpu.SMEM)
HBM = pl.BlockSpec(memory_space=pltpu.HBM)
LIMIT = 16 * 1024 * 1024


def product(terms):
    return functools.reduce(
        jnp.add, [jnp.dot(h, v, preferred_element_type=jnp.float32) for h, v in terms]
    )


def edge_kernel(rows, cols, side, field, near, far, even, odd, far_even, far_odd):
    core, parity = side[0], side[1]
    row_near, row_far = (1 - core) * (rows - 1), core * (rows - 1)
    col_even, col_odd = (1 - parity) * (cols - 1), parity * (cols - 1)
    for i in range(rows):
        even[i] = field[i, col_even]
        odd[i] = field[i, col_odd]
    for j in range(cols):
        near[j] = field[row_near, j]
        far[j] = field[row_far, j]
    far_even[...] = field[row_far, col_even]
    far_odd[...] = field[row_far, col_odd]


def lines(side, rows, cols):
    core, parity = side[0], side[1]
    lines_x = (((1 - core) * (rows - 1), 1 - 2 * core), (core * (rows - 1), 2 * core - 1))
    lines_y = (((1 - parity) * (cols - 1), 1 - 2 * parity), (parity * (cols - 1), 2 * parity - 1))
    return lines_x, lines_y


def rim_codes(side, rows, cols):
    lines_x, lines_y = lines(side, rows, cols)
    for j, b in lines_y:
        for i, a in lines_x:
            yield i, j, ((a, 0), (a, -b), (0, b), (-a, b), (a, b))
        for i in range(1, rows - 1):
            yield i, j, [(c, b) for c in (-1, 0, 1)]
    for i, a in lines_x:
        for j in range(1, cols - 1):
            yield i, j, [(a, c) for c in (-1, 0, 1)]


def first_kernel(rows, cols, listed, stored, field, ham, place, total, rounded, sems):
    copies = [pltpu.make_async_copy(stored.at[i], ham.at[i], sems.at[i]) for i in range(rows)]
    for copy in copies:
        copy.start()
    for i in range(rows):
        for j in range(cols):
            for k in range(NBR):
                place[(i * cols + j) * NBR + listed[i, j, k]] = k
    for i in range(rows):
        copies[i].wait()
        local_row(i, rows, cols, place, ham, field, None, total, rounded)


def local_kernel(chosen, rows, cols, outs, place, ham, field, before, *refs):
    total, rounded = (*refs[-outs:], None)[:2]
    for i in chosen:
        local_row(i, rows, cols, place, ham, field, before, total, rounded)


def local_row(i, rows, cols, place, ham, field, before, total, rounded):
    for j in range(cols):
        codes = [
            (a, b)
            for a in (-1, 0, 1)
            for b in (-1, 0, 1)
            if 0 <= i + a < rows and 0 <= j + b < cols
        ]
        value = product(
            [
                (ham[i, j, place[(i * cols + j) * NBR + (a + 1) * 3 + b + 1]], field[i + a, j + b])
                for a, b in codes
            ]
        )
        if before is not None:
            value = 2.0 * value - before[i, j].astype(jnp.float32)
        total[i, j] = value
        if len(codes) == NBR and rounded is not None:
            rounded[i, j] = value.astype(jnp.bfloat16)


def rim_kernel(first, last, rows, cols, place, side, ham, far, even, odd, near2, far_even, far_odd, near, partial, *refs):
    if last:
        total, stored, sems = refs
    else:
        total, rounded, send_near, send_far, send_even, send_odd, send_far_even, send_far_odd = refs[1:]
    lines_x, lines_y = lines(side, rows, cols)
    halos_x, halos_y = (near, far), (even, odd)
    corners = ((near2.at[0], near2.at[1]), (far_even, far_odd))
    cells = rim_codes(side, rows, cols)
    copies = []

    def store(*place):
        if last:
            copies.append(pltpu.make_async_copy(total.at[place], stored.at[place], sems.at[len(copies)]))
            copies[-1].start()

    def cell(fields):
        i, j, codes = next(cells)
        base = (i * cols + j) * NBR + 4
        blocks = [ham[i, j, place[base + a * 3 + b]] for a, b in codes]
        value = product(list(zip(blocks, fields)))
        value = partial[i, j] + (value if first else 2.0 * value)
        total[i, j] = value
        if last:
            return None
        value = value.astype(jnp.bfloat16)
        rounded[i, j] = value
        return value

    for i in range(1, rows - 1):
        store(i, pl.ds(1, cols - 2))
    for y, (j, b) in enumerate(lines_y):
        halo_y = halos_y[y]
        for x, (i, a) in enumerate(lines_x):
            halo_x = halos_x[x]
            value = cell((halo_x[j], halo_x[j - b], halo_y[i], halo_y[i - a], corners[x][y][...]))
            if not last:
                (send_near, send_far)[x][j] = value
                (send_even, send_odd)[y][i] = value
                if x == 1:
                    (send_far_even, send_far_odd)[y][...] = value
        for i in range(1, rows - 1):
            value = cell([halo_y[i + c] for c in (-1, 0, 1)])
            if not last:
                (send_even, send_odd)[y][i] = value
        store(pl.ds(1, rows - 2), j)
    for x, (i, a) in enumerate(lines_x):
        for j in range(1, cols - 1):
            value = cell([halos_x[x][j + c] for c in (-1, 0, 1)])
            if not last:
                (send_near, send_far)[x][j] = value
        store(i)
    for copy in copies:
        copy.wait()


def swaps(size_x, size_y):
    def pairs(move):
        out = []
        for x in range(size_x):
            for y in range(size_y):
                a, b = move(x, y)
                out.append((x * size_y + y, (a % size_x) * size_y + b % size_y))
        return out

    def far(x):
        return x - 1 + 2 * (x % 2)

    def odd(y):
        return y - 1 + 2 * (y % 2)

    return dict(
        near=pairs(lambda x, y: (x ^ 1, y)),
        far=pairs(lambda x, y: (far(x), y)),
        even=pairs(lambda x, y: (x, y ^ 1)),
        odd=pairs(lambda x, y: (x, odd(y))),
        far_even=pairs(lambda x, y: (far(x), y ^ 1)),
        far_odd=pairs(lambda x, y: (far(x), odd(y))),
    )


def on_device(vectors, hamiltonian, neighbours):
    rows, cols, size, trials = vectors.shape
    axes = ("gx", "gy")
    pairs = swaps(lax.axis_size("gx"), lax.axis_size("gy"))
    core = lax.axis_index("gx") % 2
    parity = lax.axis_index("gy") % 2
    side = jnp.stack([core, parity]).astype(jnp.int32)

    def shape(*dims, dtype=jnp.bfloat16):
        return jax.ShapeDtypeStruct((*dims, size, trials), dtype)

    sends = (shape(cols), shape(cols), shape(rows), shape(rows), shape(), shape())
    params = pltpu.CompilerParams(vmem_limit_bytes=LIMIT)

    def cost(products):
        return pl.CostEstimate(
            flops=products * 2 * size * size * trials,
            bytes_accessed=products * 2 * size * size,
            transcendentals=0,
        )

    edges = pl.pallas_call(
        functools.partial(edge_kernel, rows, cols),
        out_shape=sends,
        in_specs=[SMEM, VMEM],
        out_specs=[VMEM] * len(sends),
        compiler_params=params,
        name="edges",
    )(side, vectors)

    def depart(edges):
        names = ("near", "far", "even", "odd", "far_even", "far_odd")
        return [lax.ppermute(sent, axes, pairs[name]) for sent, name in zip(edges, names)]

    def pass_on(even, odd):
        row_near = (1 - core) * (rows - 1)
        both = jnp.stack([lax.dynamic_index_in_dim(v, row_near, keepdims=False) for v in (even, odd)])
        return lax.ppermute(both, axes, pairs["near"])

    def local(kept, chosen, *operands):
        done = len(operands) - 4
        return pl.pallas_call(
            functools.partial(local_kernel, chosen, rows, cols, len(kept)),
            out_shape=kept,
            in_specs=[SMEM] + [VMEM] * (len(operands) - 1),
            out_specs=[VMEM] * len(kept),
            input_output_aliases={4 + i: i for i in range(done)},
            compiler_params=params,
            cost_estimate=cost(55 * len(chosen)),
            name="local",
        )(*operands)

    field, before, newest = vectors, None, None
    for step in range(STEPS):
        first, last = step == 0, step == STEPS - 1
        near, far, even, odd, far_even, far_odd = depart(edges)
        both = (shape(rows, cols, dtype=jnp.float32), shape(rows, cols))
        kept = both[:1] if last else both
        if first:
            hamiltonian, place, partial, *rounded = pl.pallas_call(
                functools.partial(first_kernel, rows, cols),
                out_shape=(
                    jax.ShapeDtypeStruct(hamiltonian.shape, hamiltonian.dtype),
                    jax.ShapeDtypeStruct((neighbours.size,), jnp.int32),
                    *kept,
                ),
                in_specs=[SMEM, HBM, VMEM],
                out_specs=[VMEM, SMEM, VMEM, VMEM],
                scratch_shapes=[pltpu.SemaphoreType.DMA((rows,))],
                compiler_params=params,
                cost_estimate=cost(220),
                name="local",
            )(neighbours, pltpu.with_memory_space_constraint(hamiltonian, pltpu.HBM), field)
            near2 = pass_on(even, odd)
        else:
            fixed = (place, hamiltonian, field, before)
            begun = local(kept, range(rows), *fixed)
            even, odd, far_even, far_odd, begun = lax.optimization_barrier(
                (even, odd, far_even, far_odd, tuple(begun))
            )
            near2 = pass_on(even, odd)
            partial, *rounded = begun
        operands = (place, side, hamiltonian)
        operands += (far, even, odd, near2, far_even, far_odd, near, partial, *rounded)
        out = pl.pallas_call(
            functools.partial(rim_kernel, first, last, rows, cols),
            out_shape=kept + (kept if last else sends),
            in_specs=[SMEM] * 2 + [VMEM] * (len(operands) - 2),
            out_specs=[VMEM, HBM] if last else [VMEM] * (2 + len(sends)),
            scratch_shapes=[pltpu.SemaphoreType.DMA((rows + 2,))] if last else [],
            input_output_aliases={10: 0} if last else {10: 0, 11: 1},
            compiler_params=params,
            cost_estimate=cost(68),
            name="rim",
        )(*operands)
        if last:
            return out[1]
        total, rounded, *edges = out
        before, newest = vectors if first else newest, total
        field = rounded


def solution(mesh):
    placed = (P("gx", "gy", None, None), P("gx", "gy", None, None, None), P("gx", "gy", None))
    return jax.shard_map(
        on_device, mesh=mesh, in_specs=placed, out_specs=P("gx", "gy", None, None), check_vma=False
    )
```

time: 176 us -> 85.9 us (0.49)
  waiting for transfers between devices: 56.6 us -> 2.77 us
  matrix products: 44.4 us -> 0 us
  starting transfers between devices: 26.2 us -> 58.4 us
  local copies, waits for them, and re-layouts: 30.3 us -> 3.24 us
  Pallas kernels: 0 us -> 20.3 us
  other arithmetic: 16 us -> 0.11 us
    ppermute x16 -> x28, waiting for transfers between devices: 56.6 us -> 2.77 us  [the longest x4 2.71 us: pass_on(): return lax.ppermute(both, axes, pairs['near'])]
    dot_general x5 -> x0, matrix products: 44.4 us -> none  [the longest x4 31 us: operate(): jnp.einsum('xyoij,oxyjm->xyim', ordered, stacked, preferred_element_type=...]
    ppermute x16 -> x28, starting transfers between devices: 26.2 us -> 58.4 us  [the longest x24 51.6 us: depart(): lax.ppermute(sent, axes, pairs[name])]
    pallas_call x0 -> x9, Pallas kernels: none -> 20.3 us  [the longest x3 7.8 us: local(): pl.pallas_call(functools.partial(local_kernel, chosen, rows, cols, len(ke...]
    unnamed x35 -> x8, local copies, waits for them, and re-layouts: 18.7 us -> 3.17 us
    unnamed x14 -> x0, other arithmetic: 13 us -> none
    dot_general x1 -> x0, local copies, waits for them, and re-layouts: 8.07 us -> none  [on_device(): jnp.einsum('xyko,xykij->xyoij', onehot, hamiltonian, preferred_element_ty...]
    another operation x3 -> x0, local copies, waits for them, and re-layouts: 2.24 us -> none  [neighbour_stack(): return jnp.stack(views, axis=0)]
  transfers between devices with their start and end apart: 16 -> 28, of which waited for: 15 -> 3; matrix products, arithmetic and copies ran while one was open for 14% -> 0% of each run, Pallas kernels for 0% -> 16%
where the time goes in v2:
time: 85.9 us; the launch traced here: 85.2 us
  starting transfers between devices  58.4 us (68%)
  Pallas kernels  20.3 us (24%)
  local copies, waits for them, and re-layouts  3.24 us (4%)
  waiting for transfers between devices  2.77 us (3%)
    ppermute x24, starting transfers between devices, depart(): lax.ppermute(sent, axes, pairs[name])  51.6 us
    pallas_call x3, Pallas kernels, local(): pl.pallas_call(functools.partial(local_kernel, chosen, rows, cols, len(ke...  7.8 us
    ppermute x4, starting transfers between devices, pass_on(): return lax.ppermute(both, axes, pairs['near'])  6.75 us
    pallas_call x4, Pallas kernels, on_device(): pl.pallas_call(functools.partial(rim_kernel, first, last, rows, cols), ou...  6.26 us
    pallas_call x1, Pallas kernels, on_device(): pl.pallas_call(functools.partial(first_kernel, rows, cols), out_shape=(ja...  5.63 us
    unnamed x8, local copies, waits for them, and re-layouts  3.17 us
    ppermute x4, waiting for transfers between devices, pass_on(): return lax.ppermute(both, axes, pairs['near'])  2.71 us
  transfers between devices with their start and end apart: 28, of which 3 were waited for; matrix products, arithmetic and copies ran while one was open for 0% of the time, Pallas kernels for 16%

profile of v2, /device:TPU:1, one launch (start us, length us, event | category | flops | bytes accessed | tf_op | source)
XLA Modules:
  0.0 85.2 jit_solution(8989958977699079697)
XLA Ops:
  0.0 0.1 pad_add_fusion.side
  0.1 1.2 %copy-done = bf16[4,8,128,128]{3,2,1,0:T(8,128)(2,1)S(1)} copy-done((bf16[4,8,128,128]{3,2,1,0:T(8,128)(2,1)S(1)}, bf16[4,8,128,128]{3,2,1,0:T(8,128)(2,1)}, u32[]{:S(2)}) %copy-start) | copy-done | bytes 1048600
  1.3 0.6 edges.1
  1.9 3.7 %collective-permute-start.1 = (bf16[4,128,128]{2,1,0:T(8,128)(2,1)S(1)}, bf16[4,128,128]{2,1,0:T(8,128)(2,1)S(1)}, u32[]{:S(2)}, u32[]{:S(2)}) collective-permute-start(bf16[4,128,128]{2,1,0:T(8,128)(2,1)S(1)} %get-tuple-element.63), channel_id=1, source_target_pairs={{0,1},{1,0},{2,3},{3,2},{4,5},{5,4},{6,7},{7,6},{8,9},{9,8},{10,11... | collective-permute-start | bytes 393224 | tf_op jit(solution)/shard_map/ppermute | solution.py:210
  5.6 2.7 %collective-permute-start.2 = (bf16[4,128,128]{2,1,0:T(8,128)(2,1)S(1)}, bf16[4,128,128]{2,1,0:T(8,128)(2,1)S(1)}, u32[]{:S(2)}, u32[]{:S(2)}) collective-permute-start(bf16[4,128,128]{2,1,0:T(8,128)(2,1)S(1)} %get-tuple-element.64), channel_id=1, source_target_pairs={{0,7},{1,2},{2,1},{3,4},{4,3},{5,6},{6,5},{7,0},{8,15},{9,10},{10,... | collective-permute-start | bytes 393224 | tf_op jit(solution)/shard_map/ppermute | solution.py:210
  8.2 2.2 %collective-permute-start.4 = (bf16[128,128]{1,0:T(8,128)(2,1)S(1)}, bf16[128,128]{1,0:T(8,128)(2,1)S(1)}, u32[]{:S(2)}, u32[]{:S(2)}) collective-permute-start(bf16[128,128]{1,0:T(8,128)(2,1)S(1)} %get-tuple-element.65), channel_id=1, source_target_pairs={{0,249},{1,248},{2,251},{3,250},{4,253},{5,252},{6,255},{7,254},{8... | collective-permute-start | bytes 98312 | tf_op jit(solution)/shard_map/ppermute | solution.py:210
  10.4 1.1 %collective-permute-start.5 = (bf16[128,128]{1,0:T(8,128)(2,1)S(1)}, bf16[128,128]{1,0:T(8,128)(2,1)S(1)}, u32[]{:S(2)}, u32[]{:S(2)}) collective-permute-start(bf16[128,128]{1,0:T(8,128)(2,1)S(1)} %get-tuple-element.66), channel_id=1, source_target_pairs={{0,255},{1,250},{2,249},{3,252},{4,251},{5,254},{6,253},{7,248},{8... | collective-permute-start | bytes 98312 | tf_op jit(solution)/shard_map/ppermute | solution.py:210
  11.5 1.0 %collective-permute-start = (bf16[8,128,128]{2,1,0:T(8,128)(2,1)S(1)}, bf16[8,128,128]{2,1,0:T(8,128)(2,1)S(1)}, u32[]{:S(2)}, u32[]{:S(2)}) collective-permute-start(bf16[8,128,128]{2,1,0:T(8,128)(2,1)S(1)} %get-tuple-element.62), channel_id=1, source_target_pairs={{0,248},{1,249},{2,250},{3,251},{4,252},{5,253},{6,254},{7,255},{8... | collective-permute-start | bytes 786440 | tf_op jit(solution)/shard_map/ppermute | solution.py:210
  12.5 0.0 collective-permute-done.1.even
  12.5 6.7 %collective-permute-start.6 = (bf16[8,128,128]{2,1,0:T(8,128)(2,1)S(1)}, bf16[8,128,128]{2,1,0:T(8,128)(2,1)S(1)}, u32[]{:S(2)}, u32[]{:S(2)}) collective-permute-start(bf16[8,128,128]{2,1,0:T(8,128)(2,1)S(1)} %get-tuple-element.67), channel_id=1, source_target_pairs={{0,8},{1,9},{2,10},{3,11},{4,12},{5,13},{6,14},{7,15},{8,0},{9,1},... | collective-permute-start | bytes 786440 | tf_op jit(solution)/shard_map/ppermute | solution.py:210
  19.2 0.0 collective-permute-done.2.odd
  19.2 0.1 collective-permute-start.3
  19.3 1.2 %copy-done.1 = bf16[4,8,128,128]{3,2,1,0:T(8,128)(2,1)S(1)} copy-done((bf16[4,8,128,128]{3,2,1,0:T(8,128)(2,1)S(1)}, bf16[4,8,128,128]{3,2,1,0:T(8,128)(2,1)}, u32[]{:S(2)}) %copy-start.1) | copy-done | bytes 1048600
  20.6 0.7 copy-done.3
  21.3 5.6 %local.4 = (bf16[4,8,9,128,128]{4,3,2,1,0:T(8,128)(2,1)S(1)}, s32[288]{0:T(512)S(1)}, f32[4,8,128,128]{3,2,1,0:T(8,128)S(1)}, bf16[4,8,128,128]{3,2,1,0:T(8,128)(2,1)S(1)}) custom-call(s32[4,8,9]{2,1,0:T(8,128)S(1)} %copy-done.3, bf16[4,8,9,128,128]{4,3,2,1,0:T(8,128)(2,1)} %stored.1, bf16[4,8,128,128]{3,2,1,0:T(8,128)(2,1)S(1)} %copy-done.1), custom_call_target="tpu_custom_call" | custom-call | flops 922746880 | bytes 7208960 | tf_op jit(solution)/shard_map/local/pallas_call | solution.py:237
  26.9 0.0 collective-permute-done.4.far_even
  26.9 0.0 collective-permute-done.3.near2
  26.9 0.0 collective-permute-done.far
  27.0 0.0 copy-start.2
  27.0 1.4 %rim.4 = (f32[4,8,128,128]{3,2,1,0:T(8,128)S(1)}, bf16[4,8,128,128]{3,2,1,0:T(8,128)(2,1)S(1)}, bf16[8,128,128]{2,1,0:T(8,128)(2,1)S(1)}, bf16[8,128,128]{2,1,0:...) custom-call(s32[288]{0:T(512)S(1)} %get-tuple-element.60.place, ...), custom_call_target="tpu_custom_call", output_to_operand_aliasing={{0}: (10, {}), {1}: (11, {})} | custom-call | flops 285212672 | bytes 2228224 | tf_op jit(solution)/shard_map/rim/pallas_call | solution.py:262
  28.3 3.1 %collective-permute-start.8 = (bf16[4,128,128]{2,1,0:T(8,128)(2,1)S(1)}, bf16[4,128,128]{2,1,0:T(8,128)(2,1)S(1)}, u32[]{:S(2)}, u32[]{:S(2)}) collective-permute-start(bf16[4,128,128]{2,1,0:T(8,128)(2,1)S(1)} %get-tuple-element.71), channel_id=1, source_target_pairs={{0,1},{1,0},{2,3},{3,2},{4,5},{5,4},{6,7},{7,6},{8,9},{9,8},{10,11... | collective-permute-start | bytes 393224 | tf_op jit(solution)/shard_map/ppermute | solution.py:210
  31.5 1.2 %collective-permute-start.9 = (bf16[4,128,128]{2,1,0:T(8,128)(2,1)S(1)}, bf16[4,128,128]{2,1,0:T(8,128)(2,1)S(1)}, u32[]{:S(2)}, u32[]{:S(2)}) collective-permute-start(bf16[4,128,128]{2,1,0:T(8,128)(2,1)S(1)} %get-tuple-element.72), channel_id=1, source_target_pairs={{0,7},{1,2},{2,1},{3,4},{4,3},{5,6},{6,5},{7,0},{8,15},{9,10},{10,... | collective-permute-start | bytes 393224 | tf_op jit(solution)/shard_map/ppermute | solution.py:210
  32.7 2.9 %collective-permute-start.11 = (bf16[128,128]{1,0:T(8,128)(2,1)S(1)}, bf16[128,128]{1,0:T(8,128)(2,1)S(1)}, u32[]{:S(2)}, u32[]{:S(2)}) collective-permute-start(bf16[128,128]{1,0:T(8,128)(2,1)S(1)} %get-tuple-element.74), channel_id=1, source_target_pairs={{0,255},{1,250},{2,249},{3,252},{4,251},{5,254},{6,253},{7,248},{8... | collective-permute-start | bytes 98312 | tf_op jit(solution)/shard_map/ppermute | solution.py:210
  35.5 1.0 %collective-permute-start.7 = (bf16[8,128,128]{2,1,0:T(8,128)(2,1)S(1)}, bf16[8,128,128]{2,1,0:T(8,128)(2,1)S(1)}, u32[]{:S(2)}, u32[]{:S(2)}) collective-permute-start(bf16[8,128,128]{2,1,0:T(8,128)(2,1)S(1)} %get-tuple-element.70), channel_id=1, source_target_pairs={{0,248},{1,249},{2,250},{3,251},{4,252},{5,253},{6,254},{7,255},{8... | collective-permute-start | bytes 786440 | tf_op jit(solution)/shard_map/ppermute | solution.py:210
  36.5 2.6 %local.5 = (f32[4,8,128,128]{3,2,1,0:T(8,128)S(1)}, bf16[4,8,128,128]{3,2,1,0:T(8,128)(2,1)S(1)}) custom-call(s32[288]{0:T(512)S(1)} %get-tuple-element.60.place, bf16[4,8,9,128,128]{4,3,2,1,0:T(8,128)(2,1)S(1)} %get-tuple-element.61.ham, bf16[4,8,128,128]{3,2,1,0:T(8,128)(2,1)S(1)} %get-tuple-element.75.field, bf16[4,8,128,128]{3,2,1,0:T(8,128)(2,1)S(1)} %copy-done.2), custom_call_target="tpu_custom_call" | custom-call | flops 922746880 | bytes 7208960 | tf_op jit(solution)/shard_map/local/pallas_call | solution.py:219
  39.1 3.4 %collective-permute-start.13 = (bf16[8,128,128]{2,1,0:T(8,128)(2,1)S(1)}, bf16[8,128,128]{2,1,0:T(8,128)(2,1)S(1)}, u32[]{:S(2)}, u32[]{:S(2)}) collective-permute-start(bf16[8,128,128]{2,1,0:T(8,128)(2,1)S(1)} %get-tuple-element.82), channel_id=1, source_target_pairs={{0,8},{1,9},{2,10},{3,11},{4,12},{5,13},{6,14},{7,15},{8,0},{9,1},... | collective-permute-start | bytes 786440 | tf_op jit(solution)/shard_map/ppermute | solution.py:210
  42.6 2.0 %collective-permute-start.12 = (bf16[2,128,128]{2,1,0:T(8,128)(2,1)S(1)}, bf16[2,128,128]{2,1,0:T(8,128)(2,1)S(1)}, u32[]{:S(2)}, u32[]{:S(2)}) collective-permute-start(bf16[2,128,128]{2,1,0:T(8,128)(2,1)S(1)} %pad_maximum_fusion.1), channel_id=1, source_target_pairs={{0,8},{1,9},{2,10},{3,11},{4,12},{5,13},{6,14},{7,15},{8,0},{9,1},... | collective-permute-start | bytes 196616 | tf_op jit(solution)/shard_map/ppermute | solution.py:215
  44.6 0.9 %collective-permute-done.12.near2 = bf16[2,128,128]{2,1,0:T(8,128)(2,1)S(1)} collective-permute-done((bf16[2,128,128]{2,1,0:T(8,128)(2,1)S(1)}, bf16[2,128,128]{2,1,0:T(8,128)(2,1)S(1)}, u32[]{:S(2)}, u32[]{:S(2)}) %collective-permute-start.12) | collective-permute-done | bytes 65568 | tf_op jit(solution)/shard_map/ppermute | solution.py:215
  45.5 1.4 %rim.5 = (f32[4,8,128,128]{3,2,1,0:T(8,128)S(1)}, bf16[4,8,128,128]{3,2,1,0:T(8,128)(2,1)S(1)}, bf16[8,128,128]{2,1,0:T(8,128)(2,1)S(1)}, bf16[8,128,128]{2,1,0:...) custom-call(s32[288]{0:T(512)S(1)} %get-tuple-element.60.place, ...), custom_call_target="tpu_custom_call", output_to_operand_aliasing={{0}: (10, {}), {1}: (11, {})} | custom-call | flops 285212672 | bytes 2228224 | tf_op jit(solution)/shard_map/rim/pallas_call | solution.py:262
  46.8 1.8 %collective-permute-start.15 = (bf16[4,128,128]{2,1,0:T(8,128)(2,1)S(1)}, bf16[4,128,128]{2,1,0:T(8,128)(2,1)S(1)}, u32[]{:S(2)}, u32[]{:S(2)}) collective-permute-start(bf16[4,128,128]{2,1,0:T(8,128)(2,1)S(1)} %get-tuple-element.86), channel_id=1, source_target_pairs={{0,1},{1,0},{2,3},{3,2},{4,5},{5,4},{6,7},{7,6},{8,9},{9,8},{10,11... | collective-permute-start | bytes 393224 | tf_op jit(solution)/shard_map/ppermute | solution.py:210
  48.7 1.5 %collective-permute-start.16 = (bf16[4,128,128]{2,1,0:T(8,128)(2,1)S(1)}, bf16[4,128,128]{2,1,0:T(8,128)(2,1)S(1)}, u32[]{:S(2)}, u32[]{:S(2)}) collective-permute-start(bf16[4,128,128]{2,1,0:T(8,128)(2,1)S(1)} %get-tuple-element.87), channel_id=1, source_target_pairs={{0,7},{1,2},{2,1},{3,4},{4,3},{5,6},{6,5},{7,0},{8,15},{9,10},{10,... | collective-permute-start | bytes 393224 | tf_op jit(solution)/shard_map/ppermute | solution.py:210
  50.1 0.5 collective-permute-start.17
  50.7 2.6 %collective-permute-start.18 = (bf16[128,128]{1,0:T(8,128)(2,1)S(1)}, bf16[128,128]{1,0:T(8,128)(2,1)S(1)}, u32[]{:S(2)}, u32[]{:S(2)}) collective-permute-start(bf16[128,128]{1,0:T(8,128)(2,1)S(1)} %get-tuple-element.89), channel_id=1, source_target_pairs={{0,255},{1,250},{2,249},{3,252},{4,251},{5,254},{6,253},{7,248},{8... | collective-permute-start | bytes 98312 | tf_op jit(solution)/shard_map/ppermute | solution.py:210
  53.3 0.4 collective-permute-start.14
  53.7 2.6 %local.6 = (f32[4,8,128,128]{3,2,1,0:T(8,128)S(1)}, bf16[4,8,128,128]{3,2,1,0:T(8,128)(2,1)S(1)}) custom-call(s32[288]{0:T(512)S(1)} %get-tuple-element.60.place, bf16[4,8,9,128,128]{4,3,2,1,0:T(8,128)(2,1)S(1)} %get-tuple-element.61.ham, bf16[4,8,128,128]{3,2,1,0:T(8,128)(2,1)S(1)} %get-tuple-element.90.field, f32[4,8,128,128]{3,2,1,0:T(8,128)S(1)} %get-tuple-element.91.before), custom_call_target="tpu_custom_call" | custom-call | flops 922746880 | bytes 7208960 | tf_op jit(solution)/shard_map/local/pallas_call | solution.py:219
  56.3 4.2 %collective-permute-start.20 = (bf16[8,128,128]{2,1,0:T(8,128)(2,1)S(1)}, bf16[8,128,128]{2,1,0:T(8,128)(2,1)S(1)}, u32[]{:S(2)}, u32[]{:S(2)}) collective-permute-start(bf16[8,128,128]{2,1,0:T(8,128)(2,1)S(1)} %get-tuple-element.98), channel_id=1, source_target_pairs={{0,8},{1,9},{2,10},{3,11},{4,12},{5,13},{6,14},{7,15},{8,0},{9,1},... | collective-permute-start | bytes 786440 | tf_op jit(solution)/shard_map/ppermute | solution.py:210
  60.6 2.4 %collective-permute-start.19 = (bf16[2,128,128]{2,1,0:T(8,128)(2,1)S(1)}, bf16[2,128,128]{2,1,0:T(8,128)(2,1)S(1)}, u32[]{:S(2)}, u32[]{:S(2)}) collective-permute-start(bf16[2,128,128]{2,1,0:T(8,128)(2,1)S(1)} %pad_maximum_fusion.2), channel_id=1, source_target_pairs={{0,8},{1,9},{2,10},{3,11},{4,12},{5,13},{6,14},{7,15},{8,0},{9,1},... | collective-permute-start | bytes 196616 | tf_op jit(solution)/shard_map/ppermute | solution.py:215
  63.0 0.9 %collective-permute-done.19.near2 = bf16[2,128,128]{2,1,0:T(8,128)(2,1)S(1)} collective-permute-done((bf16[2,128,128]{2,1,0:T(8,128)(2,1)S(1)}, bf16[2,128,128]{2,1,0:T(8,128)(2,1)S(1)}, u32[]{:S(2)}, u32[]{:S(2)}) %collective-permute-start.19) | collective-permute-done | bytes 65568 | tf_op jit(solution)/shard_map/ppermute | solution.py:215
  63.9 1.3 %rim.6 = (f32[4,8,128,128]{3,2,1,0:T(8,128)S(1)}, bf16[4,8,128,128]{3,2,1,0:T(8,128)(2,1)S(1)}, bf16[8,128,128]{2,1,0:T(8,128)(2,1)S(1)}, bf16[8,128,128]{2,1,0:...) custom-call(s32[288]{0:T(512)S(1)} %get-tuple-element.60.place, ...), custom_call_target="tpu_custom_call", output_to_operand_aliasing={{0}: (10, {}), {1}: (11, {})} | custom-call | flops 285212672 | bytes 2228224 | tf_op jit(solution)/shard_map/rim/pallas_call | solution.py:262
  65.3 0.9 %collective-permute-start.22 = (bf16[4,128,128]{2,1,0:T(8,128)(2,1)S(1)}, bf16[4,128,128]{2,1,0:T(8,128)(2,1)S(1)}, u32[]{:S(2)}, u32[]{:S(2)}) collective-permute-start(bf16[4,128,128]{2,1,0:T(8,128)(2,1)S(1)} %get-tuple-element.102), channel_id=1, source_target_pairs={{0,1},{1,0},{2,3},{3,2},{4,5},{5,4},{6,7},{7,6},{8,9},{9,8},{10,11... | collective-permute-start | bytes 393224 | tf_op jit(solution)/shard_map/ppermute | solution.py:210
  66.2 3.0 %collective-permute-start.23 = (bf16[4,128,128]{2,1,0:T(8,128)(2,1)S(1)}, bf16[4,128,128]{2,1,0:T(8,128)(2,1)S(1)}, u32[]{:S(2)}, u32[]{:S(2)}) collective-permute-start(bf16[4,128,128]{2,1,0:T(8,128)(2,1)S(1)} %get-tuple-element.103), channel_id=1, source_target_pairs={{0,7},{1,2},{2,1},{3,4},{4,3},{5,6},{6,5},{7,0},{8,15},{9,10},{10,... | collective-permute-start | bytes 393224 | tf_op jit(solution)/shard_map/ppermute | solution.py:210
  69.1 2.9 %collective-permute-start.25 = (bf16[128,128]{1,0:T(8,128)(2,1)S(1)}, bf16[128,128]{1,0:T(8,128)(2,1)S(1)}, u32[]{:S(2)}, u32[]{:S(2)}) collective-permute-start(bf16[128,128]{1,0:T(8,128)(2,1)S(1)} %get-tuple-element.105), channel_id=1, source_target_pairs={{0,255},{1,250},{2,249},{3,252},{4,251},{5,254},{6,253},{7,248},{8... | collective-permute-start | bytes 98312 | tf_op jit(solution)/shard_map/ppermute | solution.py:210
  72.1 0.0 collective-permute-start.21
  72.1 2.6 %local.7.partial = f32[4,8,128,128]{3,2,1,0:T(8,128)S(1)} custom-call(s32[288]{0:T(512)S(1)} %get-tuple-element.60.place, bf16[4,8,9,128,128]{4,3,2,1,0:T(8,128)(2,1)S(1)} %get-tuple-element.61.ham, bf16[4,8,128,128]{3,2,1,0:T(8,128)(2,1)S(1)} %get-tuple-element.106.field, f32[4,8,128,128]{3,2,1,0:T(8,128)S(1)} %get-tuple-element.107.before), custom_call_target="tpu_custom_call" | custom-call | flops 922746880 | bytes 7208960 | tf_op jit(solution)/shard_map/local/pallas_call | solution.py:219
  74.7 4.9 %collective-permute-start.27 = (bf16[8,128,128]{2,1,0:T(8,128)(2,1)S(1)}, bf16[8,128,128]{2,1,0:T(8,128)(2,1)S(1)}, u32[]{:S(2)}, u32[]{:S(2)}) collective-permute-start(bf16[8,128,128]{2,1,0:T(8,128)(2,1)S(1)} %get-tuple-element.112), channel_id=1, source_target_pairs={{0,8},{1,9},{2,10},{3,11},{4,12},{5,13},{6,14},{7,15},{8,0},{9,1},... | collective-permute-start | bytes 786440 | tf_op jit(solution)/shard_map/ppermute | solution.py:210
  79.6 2.3 %collective-permute-start.26 = (bf16[2,128,128]{2,1,0:T(8,128)(2,1)S(1)}, bf16[2,128,128]{2,1,0:T(8,128)(2,1)S(1)}, u32[]{:S(2)}, u32[]{:S(2)}) collective-permute-start(bf16[2,128,128]{2,1,0:T(8,128)(2,1)S(1)} %pad_maximum_fusion.3), channel_id=1, source_target_pairs={{0,8},{1,9},{2,10},{3,11},{4,12},{5,13},{6,14},{7,15},{8,0},{9,1},... | collective-permute-start | bytes 196616 | tf_op jit(solution)/shard_map/ppermute | solution.py:215
  81.9 0.9 %collective-permute-done.26.near2 = bf16[2,128,128]{2,1,0:T(8,128)(2,1)S(1)} collective-permute-done((bf16[2,128,128]{2,1,0:T(8,128)(2,1)S(1)}, bf16[2,128,128]{2,1,0:T(8,128)(2,1)S(1)}, u32[]{:S(2)}, u32[]{:S(2)}) %collective-permute-start.26) | collective-permute-done | bytes 65568 | tf_op jit(solution)/shard_map/ppermute | solution.py:215
  82.9 2.2 %rim.7 = (f32[4,8,128,128]{3,2,1,0:T(8,128)S(1)}, f32[4,8,128,128]{3,2,1,0:T(8,128)}) custom-call(s32[288]{0:T(512)S(1)} %get-tuple-element.60.place, s32[2]{0:T(128)S(1)} %pad_add_fusion.side, bf16[4,8,9,128,128]{4,3,2,1,0:T(8,128)(2,1)S(1)} %get-tuple-element.61.ham, ...), custom_call_target="tpu_custom_call", output_to_operand_aliasing={{0}: (10, {})} | custom-call | flops 285212672 | bytes 2228224 | tf_op jit(solution)/shard_map/rim/pallas_call | solution.py:262
  (37 shorter events, 0.2 us)
Async XLA Ops:
  0.1 1.2 %copy-start = (bf16[4,8,128,128]{3,2,1,0:T(8,128)(2,1)S(1)}, bf16[4,8,128,128]{3,2,1,0:T(8,128)(2,1)}, u32[]{:S(2)}) copy-start(bf16[4,8,128,128]{3,2,1,0:T(8,128)(2,1)} %before.1) | copy-start | bytes 3145732
  1.9 10.6 %collective-permute-start.1 = (bf16[4,128,128]{2,1,0:T(8,128)(2,1)S(1)}, bf16[4,128,128]{2,1,0:T(8,128)(2,1)S(1)}, u32[]{:S(2)}, u32[]{:S(2)}) collective-permute-start(bf16[4,128,128]{2,1,0:T(8,128)(2,1)S(1)} %get-tuple-element.63), channel_id=1, source_target_pairs={{0,1},{1,0},{2,3},{3,2},{4,5},{5,4},{6,7},{7,6},{8,9},{9,8},{10,11... | collective-permute-start | bytes 393224 | tf_op jit(solution)/shard_map/ppermute | solution.py:210
  5.6 13.6 %collective-permute-start.2 = (bf16[4,128,128]{2,1,0:T(8,128)(2,1)S(1)}, bf16[4,128,128]{2,1,0:T(8,128)(2,1)S(1)}, u32[]{:S(2)}, u32[]{:S(2)}) collective-permute-start(bf16[4,128,128]{2,1,0:T(8,128)(2,1)S(1)} %get-tuple-element.64), channel_id=1, source_target_pairs={{0,7},{1,2},{2,1},{3,4},{4,3},{5,6},{6,5},{7,0},{8,15},{9,10},{10,... | collective-permute-start | bytes 393224 | tf_op jit(solution)/shard_map/ppermute | solution.py:210
  8.2 18.7 %collective-permute-start.4 = (bf16[128,128]{1,0:T(8,128)(2,1)S(1)}, bf16[128,128]{1,0:T(8,128)(2,1)S(1)}, u32[]{:S(2)}, u32[]{:S(2)}) collective-permute-start(bf16[128,128]{1,0:T(8,128)(2,1)S(1)} %get-tuple-element.65), channel_id=1, source_target_pairs={{0,249},{1,248},{2,251},{3,250},{4,253},{5,252},{6,255},{7,254},{8... | collective-permute-start | bytes 98312 | tf_op jit(solution)/shard_map/ppermute | solution.py:210
  10.4 16.5 %collective-permute-start.5 = (bf16[128,128]{1,0:T(8,128)(2,1)S(1)}, bf16[128,128]{1,0:T(8,128)(2,1)S(1)}, u32[]{:S(2)}, u32[]{:S(2)}) collective-permute-start(bf16[128,128]{1,0:T(8,128)(2,1)S(1)} %get-tuple-element.66), channel_id=1, source_target_pairs={{0,255},{1,250},{2,249},{3,252},{4,251},{5,254},{6,253},{7,248},{8... | collective-permute-start | bytes 98312 | tf_op jit(solution)/shard_map/ppermute | solution.py:210
  11.5 15.4 %collective-permute-start = (bf16[8,128,128]{2,1,0:T(8,128)(2,1)S(1)}, bf16[8,128,128]{2,1,0:T(8,128)(2,1)S(1)}, u32[]{:S(2)}, u32[]{:S(2)}) collective-permute-start(bf16[8,128,128]{2,1,0:T(8,128)(2,1)S(1)} %get-tuple-element.62), channel_id=1, source_target_pairs={{0,248},{1,249},{2,250},{3,251},{4,252},{5,253},{6,254},{7,255},{8... | collective-permute-start | bytes 786440 | tf_op jit(solution)/shard_map/ppermute | solution.py:210
  12.5 14.4 %collective-permute-start.6 = (bf16[8,128,128]{2,1,0:T(8,128)(2,1)S(1)}, bf16[8,128,128]{2,1,0:T(8,128)(2,1)S(1)}, u32[]{:S(2)}, u32[]{:S(2)}) collective-permute-start(bf16[8,128,128]{2,1,0:T(8,128)(2,1)S(1)} %get-tuple-element.67), channel_id=1, source_target_pairs={{0,8},{1,9},{2,10},{3,11},{4,12},{5,13},{6,14},{7,15},{8,0},{9,1},... | collective-permute-start | bytes 786440 | tf_op jit(solution)/shard_map/ppermute | solution.py:210
  19.2 7.7 %collective-permute-start.3 = (bf16[2,128,128]{2,1,0:T(8,128)(2,1)S(1)}, bf16[2,128,128]{2,1,0:T(8,128)(2,1)S(1)}, u32[]{:S(2)}, u32[]{:S(2)}) collective-permute-start(bf16[2,128,128]{2,1,0:T(8,128)(2,1)S(1)} %pad_maximum_fusion), channel_id=1, source_target_pairs={{0,8},{1,9},{2,10},{3,11},{4,12},{5,13},{6,14},{7,15},{8,0},{9,1},... | collective-permute-start | bytes 196616 | tf_op jit(solution)/shard_map/ppermute | solution.py:215
  19.3 1.2 %copy-start.1 = (bf16[4,8,128,128]{3,2,1,0:T(8,128)(2,1)S(1)}, bf16[4,8,128,128]{3,2,1,0:T(8,128)(2,1)}, u32[]{:S(2)}) copy-start(bf16[4,8,128,128]{3,2,1,0:T(8,128)(2,1)} %before.1) | copy-start | bytes 3145732
  20.6 0.7 copy-start.3
  27.0 9.6 %copy-start.2 = (bf16[4,8,128,128]{3,2,1,0:T(8,128)(2,1)S(1)}, bf16[4,8,128,128]{3,2,1,0:T(8,128)(2,1)}, u32[]{:S(2)}) copy-start(bf16[4,8,128,128]{3,2,1,0:T(8,128)(2,1)} %before.1) | copy-start | bytes 3145732
  28.3 14.2 %collective-permute-start.8 = (bf16[4,128,128]{2,1,0:T(8,128)(2,1)S(1)}, bf16[4,128,128]{2,1,0:T(8,128)(2,1)S(1)}, u32[]{:S(2)}, u32[]{:S(2)}) collective-permute-start(bf16[4,128,128]{2,1,0:T(8,128)(2,1)S(1)} %get-tuple-element.71), channel_id=1, source_target_pairs={{0,1},{1,0},{2,3},{3,2},{4,5},{5,4},{6,7},{7,6},{8,9},{9,8},{10,11... | collective-permute-start | bytes 393224 | tf_op jit(solution)/shard_map/ppermute | solution.py:210
  31.5 11.1 %collective-permute-start.9 = (bf16[4,128,128]{2,1,0:T(8,128)(2,1)S(1)}, bf16[4,128,128]{2,1,0:T(8,128)(2,1)S(1)}, u32[]{:S(2)}, u32[]{:S(2)}) collective-permute-start(bf16[4,128,128]{2,1,0:T(8,128)(2,1)S(1)} %get-tuple-element.72), channel_id=1, source_target_pairs={{0,7},{1,2},{2,1},{3,4},{4,3},{5,6},{6,5},{7,0},{8,15},{9,10},{10,... | collective-permute-start | bytes 393224 | tf_op jit(solution)/shard_map/ppermute | solution.py:210
  32.7 6.4 %collective-permute-start.10 = (bf16[128,128]{1,0:T(8,128)(2,1)S(1)}, bf16[128,128]{1,0:T(8,128)(2,1)S(1)}, u32[]{:S(2)}, u32[]{:S(2)}) collective-permute-start(bf16[128,128]{1,0:T(8,128)(2,1)S(1)} %get-tuple-element.73), channel_id=1, source_target_pairs={{0,249},{1,248},{2,251},{3,250},{4,253},{5,252},{6,255},{7,254},{8... | collective-permute-start | bytes 98312 | tf_op jit(solution)/shard_map/ppermute | solution.py:210
  32.7 9.9 %collective-permute-start.11 = (bf16[128,128]{1,0:T(8,128)(2,1)S(1)}, bf16[128,128]{1,0:T(8,128)(2,1)S(1)}, u32[]{:S(2)}, u32[]{:S(2)}) collective-permute-start(bf16[128,128]{1,0:T(8,128)(2,1)S(1)} %get-tuple-element.74), channel_id=1, source_target_pairs={{0,255},{1,250},{2,249},{3,252},{4,251},{5,254},{6,253},{7,248},{8... | collective-permute-start | bytes 98312 | tf_op jit(solution)/shard_map/ppermute | solution.py:210
  35.5 9.9 %collective-permute-start.7 = (bf16[8,128,128]{2,1,0:T(8,128)(2,1)S(1)}, bf16[8,128,128]{2,1,0:T(8,128)(2,1)S(1)}, u32[]{:S(2)}, u32[]{:S(2)}) collective-permute-start(bf16[8,128,128]{2,1,0:T(8,128)(2,1)S(1)} %get-tuple-element.70), channel_id=1, source_target_pairs={{0,248},{1,249},{2,250},{3,251},{4,252},{5,253},{6,254},{7,255},{8... | collective-permute-start | bytes 786440 | tf_op jit(solution)/shard_map/ppermute | solution.py:210
  39.1 6.4 %collective-permute-start.13 = (bf16[8,128,128]{2,1,0:T(8,128)(2,1)S(1)}, bf16[8,128,128]{2,1,0:T(8,128)(2,1)S(1)}, u32[]{:S(2)}, u32[]{:S(2)}) collective-permute-start(bf16[8,128,128]{2,1,0:T(8,128)(2,1)S(1)} %get-tuple-element.82), channel_id=1, source_target_pairs={{0,8},{1,9},{2,10},{3,11},{4,12},{5,13},{6,14},{7,15},{8,0},{9,1},... | collective-permute-start | bytes 786440 | tf_op jit(solution)/shard_map/ppermute | solution.py:210
  42.6 2.9 %collective-permute-start.12 = (bf16[2,128,128]{2,1,0:T(8,128)(2,1)S(1)}, bf16[2,128,128]{2,1,0:T(8,128)(2,1)S(1)}, u32[]{:S(2)}, u32[]{:S(2)}) collective-permute-start(bf16[2,128,128]{2,1,0:T(8,128)(2,1)S(1)} %pad_maximum_fusion.1), channel_id=1, source_target_pairs={{0,8},{1,9},{2,10},{3,11},{4,12},{5,13},{6,14},{7,15},{8,0},{9,1},... | collective-permute-start | bytes 196616 | tf_op jit(solution)/shard_map/ppermute | solution.py:215
  46.8 13.7 %collective-permute-start.15 = (bf16[4,128,128]{2,1,0:T(8,128)(2,1)S(1)}, bf16[4,128,128]{2,1,0:T(8,128)(2,1)S(1)}, u32[]{:S(2)}, u32[]{:S(2)}) collective-permute-start(bf16[4,128,128]{2,1,0:T(8,128)(2,1)S(1)} %get-tuple-element.86), channel_id=1, source_target_pairs={{0,1},{1,0},{2,3},{3,2},{4,5},{5,4},{6,7},{7,6},{8,9},{9,8},{10,11... | collective-permute-start | bytes 393224 | tf_op jit(solution)/shard_map/ppermute | solution.py:210
  48.7 11.9 %collective-permute-start.16 = (bf16[4,128,128]{2,1,0:T(8,128)(2,1)S(1)}, bf16[4,128,128]{2,1,0:T(8,128)(2,1)S(1)}, u32[]{:S(2)}, u32[]{:S(2)}) collective-permute-start(bf16[4,128,128]{2,1,0:T(8,128)(2,1)S(1)} %get-tuple-element.87), channel_id=1, source_target_pairs={{0,7},{1,2},{2,1},{3,4},{4,3},{5,6},{6,5},{7,0},{8,15},{9,10},{10,... | collective-permute-start | bytes 393224 | tf_op jit(solution)/shard_map/ppermute | solution.py:210
  50.1 6.2 %collective-permute-start.17 = (bf16[128,128]{1,0:T(8,128)(2,1)S(1)}, bf16[128,128]{1,0:T(8,128)(2,1)S(1)}, u32[]{:S(2)}, u32[]{:S(2)}) collective-permute-start(bf16[128,128]{1,0:T(8,128)(2,1)S(1)} %get-tuple-element.88), channel_id=1, source_target_pairs={{0,249},{1,248},{2,251},{3,250},{4,253},{5,252},{6,255},{7,254},{8... | collective-permute-start | bytes 98312 | tf_op jit(solution)/shard_map/ppermute | solution.py:210
  50.7 9.9 %collective-permute-start.18 = (bf16[128,128]{1,0:T(8,128)(2,1)S(1)}, bf16[128,128]{1,0:T(8,128)(2,1)S(1)}, u32[]{:S(2)}, u32[]{:S(2)}) collective-permute-start(bf16[128,128]{1,0:T(8,128)(2,1)S(1)} %get-tuple-element.89), channel_id=1, source_target_pairs={{0,255},{1,250},{2,249},{3,252},{4,251},{5,254},{6,253},{7,248},{8... | collective-permute-start | bytes 98312 | tf_op jit(solution)/shard_map/ppermute | solution.py:210
  53.3 10.6 %collective-permute-start.14 = (bf16[8,128,128]{2,1,0:T(8,128)(2,1)S(1)}, bf16[8,128,128]{2,1,0:T(8,128)(2,1)S(1)}, u32[]{:S(2)}, u32[]{:S(2)}) collective-permute-start(bf16[8,128,128]{2,1,0:T(8,128)(2,1)S(1)} %get-tuple-element.85), channel_id=1, source_target_pairs={{0,248},{1,249},{2,250},{3,251},{4,252},{5,253},{6,254},{7,255},{8... | collective-permute-start | bytes 786440 | tf_op jit(solution)/shard_map/ppermute | solution.py:210
  56.3 7.6 %collective-permute-start.20 = (bf16[8,128,128]{2,1,0:T(8,128)(2,1)S(1)}, bf16[8,128,128]{2,1,0:T(8,128)(2,1)S(1)}, u32[]{:S(2)}, u32[]{:S(2)}) collective-permute-start(bf16[8,128,128]{2,1,0:T(8,128)(2,1)S(1)} %get-tuple-element.98), channel_id=1, source_target_pairs={{0,8},{1,9},{2,10},{3,11},{4,12},{5,13},{6,14},{7,15},{8,0},{9,1},... | collective-permute-start | bytes 786440 | tf_op jit(solution)/shard_map/ppermute | solution.py:210
  60.6 3.3 %collective-permute-start.19 = (bf16[2,128,128]{2,1,0:T(8,128)(2,1)S(1)}, bf16[2,128,128]{2,1,0:T(8,128)(2,1)S(1)}, u32[]{:S(2)}, u32[]{:S(2)}) collective-permute-start(bf16[2,128,128]{2,1,0:T(8,128)(2,1)S(1)} %pad_maximum_fusion.2), channel_id=1, source_target_pairs={{0,8},{1,9},{2,10},{3,11},{4,12},{5,13},{6,14},{7,15},{8,0},{9,1},... | collective-permute-start | bytes 196616 | tf_op jit(solution)/shard_map/ppermute | solution.py:215
  65.3 14.3 %collective-permute-start.22 = (bf16[4,128,128]{2,1,0:T(8,128)(2,1)S(1)}, bf16[4,128,128]{2,1,0:T(8,128)(2,1)S(1)}, u32[]{:S(2)}, u32[]{:S(2)}) collective-permute-start(bf16[4,128,128]{2,1,0:T(8,128)(2,1)S(1)} %get-tuple-element.102), channel_id=1, source_target_pairs={{0,1},{1,0},{2,3},{3,2},{4,5},{5,4},{6,7},{7,6},{8,9},{9,8},{10,11... | collective-permute-start | bytes 393224 | tf_op jit(solution)/shard_map/ppermute | solution.py:210
  66.2 13.4 %collective-permute-start.23 = (bf16[4,128,128]{2,1,0:T(8,128)(2,1)S(1)}, bf16[4,128,128]{2,1,0:T(8,128)(2,1)S(1)}, u32[]{:S(2)}, u32[]{:S(2)}) collective-permute-start(bf16[4,128,128]{2,1,0:T(8,128)(2,1)S(1)} %get-tuple-element.103), channel_id=1, source_target_pairs={{0,7},{1,2},{2,1},{3,4},{4,3},{5,6},{6,5},{7,0},{8,15},{9,10},{10,... | collective-permute-start | bytes 393224 | tf_op jit(solution)/shard_map/ppermute | solution.py:210
  69.1 5.6 %collective-permute-start.24 = (bf16[128,128]{1,0:T(8,128)(2,1)S(1)}, bf16[128,128]{1,0:T(8,128)(2,1)S(1)}, u32[]{:S(2)}, u32[]{:S(2)}) collective-permute-start(bf16[128,128]{1,0:T(8,128)(2,1)S(1)} %get-tuple-element.104), channel_id=1, source_target_pairs={{0,249},{1,248},{2,251},{3,250},{4,253},{5,252},{6,255},{7,254},{8... | collective-permute-start | bytes 98312 | tf_op jit(solution)/shard_map/ppermute | solution.py:210
  69.1 10.4 %collective-permute-start.25 = (bf16[128,128]{1,0:T(8,128)(2,1)S(1)}, bf16[128,128]{1,0:T(8,128)(2,1)S(1)}, u32[]{:S(2)}, u32[]{:S(2)}) collective-permute-start(bf16[128,128]{1,0:T(8,128)(2,1)S(1)} %get-tuple-element.105), channel_id=1, source_target_pairs={{0,255},{1,250},{2,249},{3,252},{4,251},{5,254},{6,253},{7,248},{8... | collective-permute-start | bytes 98312 | tf_op jit(solution)/shard_map/ppermute | solution.py:210
  72.1 10.8 %collective-permute-start.21 = (bf16[8,128,128]{2,1,0:T(8,128)(2,1)S(1)}, bf16[8,128,128]{2,1,0:T(8,128)(2,1)S(1)}, u32[]{:S(2)}, u32[]{:S(2)}) collective-permute-start(bf16[8,128,128]{2,1,0:T(8,128)(2,1)S(1)} %get-tuple-element.101), channel_id=1, source_target_pairs={{0,248},{1,249},{2,250},{3,251},{4,252},{5,253},{6,254},{7,255},{8... | collective-permute-start | bytes 786440 | tf_op jit(solution)/shard_map/ppermute | solution.py:210
  74.7 8.2 %collective-permute-start.27 = (bf16[8,128,128]{2,1,0:T(8,128)(2,1)S(1)}, bf16[8,128,128]{2,1,0:T(8,128)(2,1)S(1)}, u32[]{:S(2)}, u32[]{:S(2)}) collective-permute-start(bf16[8,128,128]{2,1,0:T(8,128)(2,1)S(1)} %get-tuple-element.112), channel_id=1, source_target_pairs={{0,8},{1,9},{2,10},{3,11},{4,12},{5,13},{6,14},{7,15},{8,0},{9,1},... | collective-permute-start | bytes 786440 | tf_op jit(solution)/shard_map/ppermute | solution.py:210
  79.6 3.2 %collective-permute-start.26 = (bf16[2,128,128]{2,1,0:T(8,128)(2,1)S(1)}, bf16[2,128,128]{2,1,0:T(8,128)(2,1)S(1)}, u32[]{:S(2)}, u32[]{:S(2)}) collective-permute-start(bf16[2,128,128]{2,1,0:T(8,128)(2,1)S(1)} %pad_maximum_fusion.3), channel_id=1, source_target_pairs={{0,8},{1,9},{2,10},{3,11},{4,12},{5,13},{6,14},{7,15},{8,0},{9,1},... | collective-permute-start | bytes 196616 | tf_op jit(solution)/shard_map/ppermute | solution.py:215

commit v3 on v2

--- a/solution.py
+++ b/solution.py
@@ -54,7 +54,9 @@
             yield i, j, [(a, c) for c in (-1, 0, 1)]
 
 
-def first_kernel(rows, cols, listed, stored, field, ham, place, total, rounded, sems):
+def first_kernel(rows, cols, listed, stored, vectors, ham, place, total, rounded, field, sems):
+    fetch = pltpu.make_async_copy(vectors, field, sems.at[rows])
+    fetch.start()
     copies = [pltpu.make_async_copy(stored.at[i], ham.at[i], sems.at[i]) for i in range(rows)]
     for copy in copies:
         copy.start()
@@ -62,6 +64,7 @@
         for j in range(cols):
             for k in range(NBR):
                 place[(i * cols + j) * NBR + listed[i, j, k]] = k
+    fetch.wait()
     for i in range(rows):
         copies[i].wait()
         local_row(i, rows, cols, place, ham, field, None, total, rounded)
@@ -241,22 +244,29 @@
                     jax.ShapeDtypeStruct((neighbours.size,), jnp.int32),
                     *kept,
                 ),
-                in_specs=[SMEM, HBM, VMEM],
+                in_specs=[SMEM, HBM, HBM],
                 out_specs=[VMEM, SMEM, VMEM, VMEM],
-                scratch_shapes=[pltpu.SemaphoreType.DMA((rows,))],
+                scratch_shapes=[
+                    pltpu.VMEM(field.shape, field.dtype),
+                    pltpu.SemaphoreType.DMA((rows + 1,)),
+                ],
                 compiler_params=params,
                 cost_estimate=cost(220),
                 name="local",
-            )(neighbours, pltpu.with_memory_space_constraint(hamiltonian, pltpu.HBM), field)
+            )(
+                neighbours,
+                pltpu.with_memory_space_constraint(hamiltonian, pltpu.HBM),
+                pltpu.with_memory_space_constraint(field, pltpu.HBM),
+            )
             near2 = pass_on(even, odd)
         else:
             fixed = (place, hamiltonian, field, before)
-            begun = local(kept, range(rows), *fixed)
+            begun = local(kept, range(0, rows - 1), *fixed)
             even, odd, far_even, far_odd, begun = lax.optimization_barrier(
                 (even, odd, far_even, far_odd, tuple(begun))
             )
             near2 = pass_on(even, odd)
-            partial, *rounded = begun
+            partial, *rounded = local(kept, range(rows - 1, rows), *fixed, *begun)
         operands = (place, side, hamiltonian)
         operands += (far, even, odd, near2, far_even, far_odd, near, partial, *rounded)
         out = pl.pallas_call(

time: 85.9 us -> 84.9 us (0.988)
  waiting for transfers between devices: 2.77 us -> 0.11 us
  Pallas kernels: 20.3 us -> 22.8 us
  local copies, waits for them, and re-layouts: 3.24 us -> 2 us
    ppermute x4, waiting for transfers between devices: 2.71 us -> 0.01 us  [pass_on(): return lax.ppermute(both, axes, pairs['near'])]
    pallas_call x3 -> x6, Pallas kernels: 7.8 us -> 10 us  [local(): pl.pallas_call(functools.partial(local_kernel, chosen, rows, cols, len(ke...]
    unnamed x8 -> x6, local copies, waits for them, and re-layouts: 3.17 us -> 1.95 us
    ppermute x4, starting transfers between devices: 6.75 us -> 7.82 us  [pass_on(): return lax.ppermute(both, axes, pairs['near'])]
  transfers between devices with their start and end apart: 28 -> 28, of which waited for: 3 -> 0; matrix products, arithmetic and copies ran while one was open for 0% -> 0% of each run, Pallas kernels for 16% -> 19%
where the time goes in v3:
time: 84.9 us; the launch traced here: 84.2 us
  starting transfers between devices  58.6 us (69%)
  Pallas kernels  22.8 us (27%)
  local copies, waits for them, and re-layouts  2 us (2%)
    ppermute x24, starting transfers between devices, depart(): lax.ppermute(sent, axes, pairs[name])  50.8 us
    pallas_call x6, Pallas kernels, local(): pl.pallas_call(functools.partial(local_kernel, chosen, rows, cols, len(ke...  10 us
    ppermute x4, starting transfers between devices, pass_on(): return lax.ppermute(both, axes, pairs['near'])  7.82 us
    pallas_call x4, Pallas kernels, on_device(): pl.pallas_call(functools.partial(rim_kernel, first, last, rows, cols), ou...  6.26 us
    pallas_call x1, Pallas kernels, on_device(): pl.pallas_call(functools.partial(first_kernel, rows, cols), out_shape=(ja...  5.98 us
    unnamed x6, local copies, waits for them, and re-layouts  1.95 us
  transfers between devices with their start and end apart: 28, of which 0 were waited for; matrix products, arithmetic and copies ran while one was open for 0% of the time, Pallas kernels for 19%

profile of v3, /device:TPU:1, one launch (start us, length us, event | category | flops | bytes accessed | tf_op | source)
XLA Modules:
  0.0 84.2 jit_solution(6015356088807947876)
XLA Ops:
  0.0 0.1 pad_add_fusion.side
  0.1 1.2 %copy-done = bf16[4,8,128,128]{3,2,1,0:T(8,128)(2,1)S(1)} copy-done((bf16[4,8,128,128]{3,2,1,0:T(8,128)(2,1)S(1)}, bf16[4,8,128,128]{3,2,1,0:T(8,128)(2,1)}, u32[]{:S(2)}) %copy-start) | copy-done | bytes 1048600
  1.3 0.6 edges.1
  1.9 3.7 %collective-permute-start.1 = (bf16[4,128,128]{2,1,0:T(8,128)(2,1)S(1)}, bf16[4,128,128]{2,1,0:T(8,128)(2,1)S(1)}, u32[]{:S(2)}, u32[]{:S(2)}) collective-permute-start(bf16[4,128,128]{2,1,0:T(8,128)(2,1)S(1)} %get-tuple-element.67), channel_id=1, source_target_pairs={{0,1},{1,0},{2,3},{3,2},{4,5},{5,4},{6,7},{7,6},{8,9},{9,8},{10,11... | collective-permute-start | bytes 393224 | tf_op jit(solution)/shard_map/ppermute | solution.py:213
  5.6 2.7 %collective-permute-start.2 = (bf16[4,128,128]{2,1,0:T(8,128)(2,1)S(1)}, bf16[4,128,128]{2,1,0:T(8,128)(2,1)S(1)}, u32[]{:S(2)}, u32[]{:S(2)}) collective-permute-start(bf16[4,128,128]{2,1,0:T(8,128)(2,1)S(1)} %get-tuple-element.68), channel_id=1, source_target_pairs={{0,7},{1,2},{2,1},{3,4},{4,3},{5,6},{6,5},{7,0},{8,15},{9,10},{10,... | collective-permute-start | bytes 393224 | tf_op jit(solution)/shard_map/ppermute | solution.py:213
  8.2 2.2 %collective-permute-start.4 = (bf16[128,128]{1,0:T(8,128)(2,1)S(1)}, bf16[128,128]{1,0:T(8,128)(2,1)S(1)}, u32[]{:S(2)}, u32[]{:S(2)}) collective-permute-start(bf16[128,128]{1,0:T(8,128)(2,1)S(1)} %get-tuple-element.69), channel_id=1, source_target_pairs={{0,249},{1,248},{2,251},{3,250},{4,253},{5,252},{6,255},{7,254},{8... | collective-permute-start | bytes 98312 | tf_op jit(solution)/shard_map/ppermute | solution.py:213
  10.4 1.1 %collective-permute-start.5 = (bf16[128,128]{1,0:T(8,128)(2,1)S(1)}, bf16[128,128]{1,0:T(8,128)(2,1)S(1)}, u32[]{:S(2)}, u32[]{:S(2)}) collective-permute-start(bf16[128,128]{1,0:T(8,128)(2,1)S(1)} %get-tuple-element.70), channel_id=1, source_target_pairs={{0,255},{1,250},{2,249},{3,252},{4,251},{5,254},{6,253},{7,248},{8... | collective-permute-start | bytes 98312 | tf_op jit(solution)/shard_map/ppermute | solution.py:213
  11.5 1.0 %collective-permute-start = (bf16[8,128,128]{2,1,0:T(8,128)(2,1)S(1)}, bf16[8,128,128]{2,1,0:T(8,128)(2,1)S(1)}, u32[]{:S(2)}, u32[]{:S(2)}) collective-permute-start(bf16[8,128,128]{2,1,0:T(8,128)(2,1)S(1)} %get-tuple-element.66), channel_id=1, source_target_pairs={{0,248},{1,249},{2,250},{3,251},{4,252},{5,253},{6,254},{7,255},{8... | collective-permute-start | bytes 786440 | tf_op jit(solution)/shard_map/ppermute | solution.py:213
  12.5 6.7 %collective-permute-start.6 = (bf16[8,128,128]{2,1,0:T(8,128)(2,1)S(1)}, bf16[8,128,128]{2,1,0:T(8,128)(2,1)S(1)}, u32[]{:S(2)}, u32[]{:S(2)}) collective-permute-start(bf16[8,128,128]{2,1,0:T(8,128)(2,1)S(1)} %get-tuple-element.71), channel_id=1, source_target_pairs={{0,8},{1,9},{2,10},{3,11},{4,12},{5,13},{6,14},{7,15},{8,0},{9,1},... | collective-permute-start | bytes 786440 | tf_op jit(solution)/shard_map/ppermute | solution.py:213
  19.2 0.1 collective-permute-start.3
  19.3 0.7 copy-done.2
  20.0 6.0 %local.7 = (bf16[4,8,9,128,128]{4,3,2,1,0:T(8,128)(2,1)S(1)}, s32[288]{0:T(512)S(1)}, f32[4,8,128,128]{3,2,1,0:T(8,128)S(1)}, bf16[4,8,128,128]{3,2,1,0:T(8,128)(2,1)S(1)}) custom-call(s32[4,8,9]{2,1,0:T(8,128)S(1)} %copy-done.2, bf16[4,8,9,128,128]{4,3,2,1,0:T(8,128)(2,1)} %stored.1, bf16[4,8,128,128]{3,2,1,0:T(8,128)(2,1)} %before.3), custom_call_target="tpu_custom_call" | custom-call | flops 922746880 | bytes 7208960 | tf_op jit(solution)/shard_map/local/pallas_call | solution.py:240
  26.0 0.0 collective-permute-done.5.far_odd
  26.1 0.0 collective-permute-done.6.near
  26.1 0.0 copy-start.1
  26.1 1.4 %rim.4 = (f32[4,8,128,128]{3,2,1,0:T(8,128)S(1)}, bf16[4,8,128,128]{3,2,1,0:T(8,128)(2,1)S(1)}, bf16[8,128,128]{2,1,0:T(8,128)(2,1)S(1)}, bf16[8,128,128]{2,1,0:...) custom-call(s32[288]{0:T(512)S(1)} %get-tuple-element.64.place, ...), custom_call_target="tpu_custom_call", output_to_operand_aliasing={{0}: (10, {}), {1}: (11, {})} | custom-call | flops 285212672 | bytes 2228224 | tf_op jit(solution)/shard_map/rim/pallas_call | solution.py:272
  27.5 3.1 %collective-permute-start.8 = (bf16[4,128,128]{2,1,0:T(8,128)(2,1)S(1)}, bf16[4,128,128]{2,1,0:T(8,128)(2,1)S(1)}, u32[]{:S(2)}, u32[]{:S(2)}) collective-permute-start(bf16[4,128,128]{2,1,0:T(8,128)(2,1)S(1)} %get-tuple-element.75), channel_id=1, source_target_pairs={{0,1},{1,0},{2,3},{3,2},{4,5},{5,4},{6,7},{7,6},{8,9},{9,8},{10,11... | collective-permute-start | bytes 393224 | tf_op jit(solution)/shard_map/ppermute | solution.py:213
  30.6 1.2 %collective-permute-start.9 = (bf16[4,128,128]{2,1,0:T(8,128)(2,1)S(1)}, bf16[4,128,128]{2,1,0:T(8,128)(2,1)S(1)}, u32[]{:S(2)}, u32[]{:S(2)}) collective-permute-start(bf16[4,128,128]{2,1,0:T(8,128)(2,1)S(1)} %get-tuple-element.76), channel_id=1, source_target_pairs={{0,7},{1,2},{2,1},{3,4},{4,3},{5,6},{6,5},{7,0},{8,15},{9,10},{10,... | collective-permute-start | bytes 393224 | tf_op jit(solution)/shard_map/ppermute | solution.py:213
  31.8 2.9 %collective-permute-start.11 = (bf16[128,128]{1,0:T(8,128)(2,1)S(1)}, bf16[128,128]{1,0:T(8,128)(2,1)S(1)}, u32[]{:S(2)}, u32[]{:S(2)}) collective-permute-start(bf16[128,128]{1,0:T(8,128)(2,1)S(1)} %get-tuple-element.78), channel_id=1, source_target_pairs={{0,255},{1,250},{2,249},{3,252},{4,251},{5,254},{6,253},{7,248},{8... | collective-permute-start | bytes 98312 | tf_op jit(solution)/shard_map/ppermute | solution.py:213
  34.7 1.0 %collective-permute-start.7 = (bf16[8,128,128]{2,1,0:T(8,128)(2,1)S(1)}, bf16[8,128,128]{2,1,0:T(8,128)(2,1)S(1)}, u32[]{:S(2)}, u32[]{:S(2)}) collective-permute-start(bf16[8,128,128]{2,1,0:T(8,128)(2,1)S(1)} %get-tuple-element.74), channel_id=1, source_target_pairs={{0,248},{1,249},{2,250},{3,251},{4,252},{5,253},{6,254},{7,255},{8... | collective-permute-start | bytes 786440 | tf_op jit(solution)/shard_map/ppermute | solution.py:213
  35.7 2.2 %local.8 = (f32[4,8,128,128]{3,2,1,0:T(8,128)S(1)}, bf16[4,8,128,128]{3,2,1,0:T(8,128)(2,1)S(1)}) custom-call(s32[288]{0:T(512)S(1)} %get-tuple-element.64.place, bf16[4,8,9,128,128]{4,3,2,1,0:T(8,128)(2,1)S(1)} %get-tuple-element.65.ham, bf16[4,8,128,128]{3,2,1,0:T(8,128)(2,1)S(1)} %get-tuple-element.79.field, bf16[4,8,128,128]{3,2,1,0:T(8,128)(2,1)S(1)} %copy-done.1), custom_call_target="tpu_custom_call" | custom-call | flops 692060160 | bytes 5406720 | tf_op jit(solution)/shard_map/local/pallas_call | solution.py:222
  37.9 0.0 collective-permute-done.10.far_even
  37.9 3.2 %collective-permute-start.13 = (bf16[8,128,128]{2,1,0:T(8,128)(2,1)S(1)}, bf16[8,128,128]{2,1,0:T(8,128)(2,1)S(1)}, u32[]{:S(2)}, u32[]{:S(2)}) collective-permute-start(bf16[8,128,128]{2,1,0:T(8,128)(2,1)S(1)} %get-tuple-element.86), channel_id=1, source_target_pairs={{0,8},{1,9},{2,10},{3,11},{4,12},{5,13},{6,14},{7,15},{8,0},{9,1},... | collective-permute-start | bytes 786440 | tf_op jit(solution)/shard_map/ppermute | solution.py:213
  41.2 2.7 %collective-permute-start.12 = (bf16[2,128,128]{2,1,0:T(8,128)(2,1)S(1)}, bf16[2,128,128]{2,1,0:T(8,128)(2,1)S(1)}, u32[]{:S(2)}, u32[]{:S(2)}) collective-permute-start(bf16[2,128,128]{2,1,0:T(8,128)(2,1)S(1)} %pad_maximum_fusion.1), channel_id=1, source_target_pairs={{0,8},{1,9},{2,10},{3,11},{4,12},{5,13},{6,14},{7,15},{8,0},{9,1},... | collective-permute-start | bytes 196616 | tf_op jit(solution)/shard_map/ppermute | solution.py:218
  43.9 1.1 %local.9 = (f32[4,8,128,128]{3,2,1,0:T(8,128)S(1)}, bf16[4,8,128,128]{3,2,1,0:T(8,128)(2,1)S(1)}) custom-call(s32[288]{0:T(512)S(1)} %get-tuple-element.64.place, bf16[4,8,9,128,128]{4,3,2,1,0:T(8,128)(2,1)S(1)} %get-tuple-element.65.ham, bf16[4,8,128,128]{3,2,1,0:T(8,128)(2,1)S(1)} %get-tuple-element.79.field, ...), custom_call_target="tpu_custom_call", output_to_operand_aliasing={{0}: (4, {}), {1}: (5, {})} | custom-call | flops 230686720 | bytes 1802240 | tf_op jit(solution)/shard_map/local/pallas_call | solution.py:222
  45.0 0.0 collective-permute-done.13.near
  45.0 1.4 %rim.5 = (f32[4,8,128,128]{3,2,1,0:T(8,128)S(1)}, bf16[4,8,128,128]{3,2,1,0:T(8,128)(2,1)S(1)}, bf16[8,128,128]{2,1,0:T(8,128)(2,1)S(1)}, bf16[8,128,128]{2,1,0:...) custom-call(s32[288]{0:T(512)S(1)} %get-tuple-element.64.place, ...), custom_call_target="tpu_custom_call", output_to_operand_aliasing={{0}: (10, {}), {1}: (11, {})} | custom-call | flops 285212672 | bytes 2228224 | tf_op jit(solution)/shard_map/rim/pallas_call | solution.py:272
  46.4 1.9 %collective-permute-start.15 = (bf16[4,128,128]{2,1,0:T(8,128)(2,1)S(1)}, bf16[4,128,128]{2,1,0:T(8,128)(2,1)S(1)}, u32[]{:S(2)}, u32[]{:S(2)}) collective-permute-start(bf16[4,128,128]{2,1,0:T(8,128)(2,1)S(1)} %get-tuple-element.92), channel_id=1, source_target_pairs={{0,1},{1,0},{2,3},{3,2},{4,5},{5,4},{6,7},{7,6},{8,9},{9,8},{10,11... | collective-permute-start | bytes 393224 | tf_op jit(solution)/shard_map/ppermute | solution.py:213
  48.2 1.4 %collective-permute-start.16 = (bf16[4,128,128]{2,1,0:T(8,128)(2,1)S(1)}, bf16[4,128,128]{2,1,0:T(8,128)(2,1)S(1)}, u32[]{:S(2)}, u32[]{:S(2)}) collective-permute-start(bf16[4,128,128]{2,1,0:T(8,128)(2,1)S(1)} %get-tuple-element.93), channel_id=1, source_target_pairs={{0,7},{1,2},{2,1},{3,4},{4,3},{5,6},{6,5},{7,0},{8,15},{9,10},{10,... | collective-permute-start | bytes 393224 | tf_op jit(solution)/shard_map/ppermute | solution.py:213
  49.7 0.1 collective-permute-start.17
  49.8 3.0 %collective-permute-start.18 = (bf16[128,128]{1,0:T(8,128)(2,1)S(1)}, bf16[128,128]{1,0:T(8,128)(2,1)S(1)}, u32[]{:S(2)}, u32[]{:S(2)}) collective-permute-start(bf16[128,128]{1,0:T(8,128)(2,1)S(1)} %get-tuple-element.95), channel_id=1, source_target_pairs={{0,255},{1,250},{2,249},{3,252},{4,251},{5,254},{6,253},{7,248},{8... | collective-permute-start | bytes 98312 | tf_op jit(solution)/shard_map/ppermute | solution.py:213
  52.8 0.5 collective-permute-start.14
  53.3 2.3 %local.10 = (f32[4,8,128,128]{3,2,1,0:T(8,128)S(1)}, bf16[4,8,128,128]{3,2,1,0:T(8,128)(2,1)S(1)}) custom-call(s32[288]{0:T(512)S(1)} %get-tuple-element.64.place, bf16[4,8,9,128,128]{4,3,2,1,0:T(8,128)(2,1)S(1)} %get-tuple-element.65.ham, bf16[4,8,128,128]{3,2,1,0:T(8,128)(2,1)S(1)} %get-tuple-element.96.field, f32[4,8,128,128]{3,2,1,0:T(8,128)S(1)} %get-tuple-element.97.before), custom_call_target="tpu_custom_call" | custom-call | flops 692060160 | bytes 5406720 | tf_op jit(solution)/shard_map/local/pallas_call | solution.py:222
  55.5 0.0 collective-permute-done.17.far_even
  55.6 3.8 %collective-permute-start.20 = (bf16[8,128,128]{2,1,0:T(8,128)(2,1)S(1)}, bf16[8,128,128]{2,1,0:T(8,128)(2,1)S(1)}, u32[]{:S(2)}, u32[]{:S(2)}) collective-permute-start(bf16[8,128,128]{2,1,0:T(8,128)(2,1)S(1)} %get-tuple-element.104), channel_id=1, source_target_pairs={{0,8},{1,9},{2,10},{3,11},{4,12},{5,13},{6,14},{7,15},{8,0},{9,1},... | collective-permute-start | bytes 786440 | tf_op jit(solution)/shard_map/ppermute | solution.py:213
  59.4 0.0 collective-permute-done.18.far_odd
  59.4 0.0 collective-permute-done.16.odd
  59.4 2.7 %collective-permute-start.19 = (bf16[2,128,128]{2,1,0:T(8,128)(2,1)S(1)}, bf16[2,128,128]{2,1,0:T(8,128)(2,1)S(1)}, u32[]{:S(2)}, u32[]{:S(2)}) collective-permute-start(bf16[2,128,128]{2,1,0:T(8,128)(2,1)S(1)} %pad_maximum_fusion.2), channel_id=1, source_target_pairs={{0,8},{1,9},{2,10},{3,11},{4,12},{5,13},{6,14},{7,15},{8,0},{9,1},... | collective-permute-start | bytes 196616 | tf_op jit(solution)/shard_map/ppermute | solution.py:218
  62.1 1.1 %local.11 = (f32[4,8,128,128]{3,2,1,0:T(8,128)S(1)}, bf16[4,8,128,128]{3,2,1,0:T(8,128)(2,1)S(1)}) custom-call(s32[288]{0:T(512)S(1)} %get-tuple-element.64.place, bf16[4,8,9,128,128]{4,3,2,1,0:T(8,128)(2,1)S(1)} %get-tuple-element.65.ham, bf16[4,8,128,128]{3,2,1,0:T(8,128)(2,1)S(1)} %get-tuple-element.96.field, ...), custom_call_target="tpu_custom_call", output_to_operand_aliasing={{0}: (4, {}), {1}: (5, {})} | custom-call | flops 230686720 | bytes 1802240 | tf_op jit(solution)/shard_map/local/pallas_call | solution.py:222
  63.3 1.4 %rim.6 = (f32[4,8,128,128]{3,2,1,0:T(8,128)S(1)}, bf16[4,8,128,128]{3,2,1,0:T(8,128)(2,1)S(1)}, bf16[8,128,128]{2,1,0:T(8,128)(2,1)S(1)}, bf16[8,128,128]{2,1,0:...) custom-call(s32[288]{0:T(512)S(1)} %get-tuple-element.64.place, ...), custom_call_target="tpu_custom_call", output_to_operand_aliasing={{0}: (10, {}), {1}: (11, {})} | custom-call | flops 285212672 | bytes 2228224 | tf_op jit(solution)/shard_map/rim/pallas_call | solution.py:272
  64.6 0.3 collective-permute-start.22
  64.9 3.5 %collective-permute-start.23 = (bf16[4,128,128]{2,1,0:T(8,128)(2,1)S(1)}, bf16[4,128,128]{2,1,0:T(8,128)(2,1)S(1)}, u32[]{:S(2)}, u32[]{:S(2)}) collective-permute-start(bf16[4,128,128]{2,1,0:T(8,128)(2,1)S(1)} %get-tuple-element.111), channel_id=1, source_target_pairs={{0,7},{1,2},{2,1},{3,4},{4,3},{5,6},{6,5},{7,0},{8,15},{9,10},{10,... | collective-permute-start | bytes 393224 | tf_op jit(solution)/shard_map/ppermute | solution.py:213
  68.5 3.0 %collective-permute-start.25 = (bf16[128,128]{1,0:T(8,128)(2,1)S(1)}, bf16[128,128]{1,0:T(8,128)(2,1)S(1)}, u32[]{:S(2)}, u32[]{:S(2)}) collective-permute-start(bf16[128,128]{1,0:T(8,128)(2,1)S(1)} %get-tuple-element.113), channel_id=1, source_target_pairs={{0,255},{1,250},{2,249},{3,252},{4,251},{5,254},{6,253},{7,248},{8... | collective-permute-start | bytes 98312 | tf_op jit(solution)/shard_map/ppermute | solution.py:213
  71.4 2.3 %local.12.refs_0_ = f32[4,8,128,128]{3,2,1,0:T(8,128)S(1)} custom-call(s32[288]{0:T(512)S(1)} %get-tuple-element.64.place, bf16[4,8,9,128,128]{4,3,2,1,0:T(8,128)(2,1)S(1)} %get-tuple-element.65.ham, bf16[4,8,128,128]{3,2,1,0:T(8,128)(2,1)S(1)} %get-tuple-element.114.field, f32[4,8,128,128]{3,2,1,0:T(8,128)S(1)} %get-tuple-element.115.before), custom_call_target="tpu_custom_call" | custom-call | flops 692060160 | bytes 5406720 | tf_op jit(solution)/shard_map/local/pallas_call | solution.py:222
  73.7 4.6 %collective-permute-start.27 = (bf16[8,128,128]{2,1,0:T(8,128)(2,1)S(1)}, bf16[8,128,128]{2,1,0:T(8,128)(2,1)S(1)}, u32[]{:S(2)}, u32[]{:S(2)}) collective-permute-start(bf16[8,128,128]{2,1,0:T(8,128)(2,1)S(1)} %get-tuple-element.120), channel_id=1, source_target_pairs={{0,8},{1,9},{2,10},{3,11},{4,12},{5,13},{6,14},{7,15},{8,0},{9,1},... | collective-permute-start | bytes 786440 | tf_op jit(solution)/shard_map/ppermute | solution.py:213
  78.3 2.4 %collective-permute-start.26 = (bf16[2,128,128]{2,1,0:T(8,128)(2,1)S(1)}, bf16[2,128,128]{2,1,0:T(8,128)(2,1)S(1)}, u32[]{:S(2)}, u32[]{:S(2)}) collective-permute-start(bf16[2,128,128]{2,1,0:T(8,128)(2,1)S(1)} %pad_maximum_fusion.3), channel_id=1, source_target_pairs={{0,8},{1,9},{2,10},{3,11},{4,12},{5,13},{6,14},{7,15},{8,0},{9,1},... | collective-permute-start | bytes 196616 | tf_op jit(solution)/shard_map/ppermute | solution.py:218
  80.7 1.1 %local.13.partial = f32[4,8,128,128]{3,2,1,0:T(8,128)S(1)} custom-call(s32[288]{0:T(512)S(1)} %get-tuple-element.64.place, bf16[4,8,9,128,128]{4,3,2,1,0:T(8,128)(2,1)S(1)} %get-tuple-element.65.ham, bf16[4,8,128,128]{3,2,1,0:T(8,128)(2,1)S(1)} %get-tuple-element.114.field, ...), custom_call_target="tpu_custom_call", output_to_operand_aliasing={{}: (4, {})} | custom-call | flops 230686720 | bytes 1802240 | tf_op jit(solution)/shard_map/local/pallas_call | solution.py:222
  81.8 2.2 %rim.7 = (f32[4,8,128,128]{3,2,1,0:T(8,128)S(1)}, f32[4,8,128,128]{3,2,1,0:T(8,128)}) custom-call(s32[288]{0:T(512)S(1)} %get-tuple-element.64.place, s32[2]{0:T(128)S(1)} %pad_add_fusion.side, bf16[4,8,9,128,128]{4,3,2,1,0:T(8,128)(2,1)S(1)} %get-tuple-element.65.ham, ...), custom_call_target="tpu_custom_call", output_to_operand_aliasing={{0}: (10, {})} | custom-call | flops 285212672 | bytes 2228224 | tf_op jit(solution)/shard_map/rim/pallas_call | solution.py:272
  (38 shorter events, 0.2 us)
Async XLA Ops:
  0.1 1.2 %copy-start = (bf16[4,8,128,128]{3,2,1,0:T(8,128)(2,1)S(1)}, bf16[4,8,128,128]{3,2,1,0:T(8,128)(2,1)}, u32[]{:S(2)}) copy-start(bf16[4,8,128,128]{3,2,1,0:T(8,128)(2,1)} %before.3) | copy-start | bytes 3145732
  1.9 10.6 %collective-permute-start.1 = (bf16[4,128,128]{2,1,0:T(8,128)(2,1)S(1)}, bf16[4,128,128]{2,1,0:T(8,128)(2,1)S(1)}, u32[]{:S(2)}, u32[]{:S(2)}) collective-permute-start(bf16[4,128,128]{2,1,0:T(8,128)(2,1)S(1)} %get-tuple-element.67), channel_id=1, source_target_pairs={{0,1},{1,0},{2,3},{3,2},{4,5},{5,4},{6,7},{7,6},{8,9},{9,8},{10,11... | collective-permute-start | bytes 393224 | tf_op jit(solution)/shard_map/ppermute | solution.py:213
  5.6 13.6 %collective-permute-start.2 = (bf16[4,128,128]{2,1,0:T(8,128)(2,1)S(1)}, bf16[4,128,128]{2,1,0:T(8,128)(2,1)S(1)}, u32[]{:S(2)}, u32[]{:S(2)}) collective-permute-start(bf16[4,128,128]{2,1,0:T(8,128)(2,1)S(1)} %get-tuple-element.68), channel_id=1, source_target_pairs={{0,7},{1,2},{2,1},{3,4},{4,3},{5,6},{6,5},{7,0},{8,15},{9,10},{10,... | collective-permute-start | bytes 393224 | tf_op jit(solution)/shard_map/ppermute | solution.py:213
  8.2 17.8 %collective-permute-start.4 = (bf16[128,128]{1,0:T(8,128)(2,1)S(1)}, bf16[128,128]{1,0:T(8,128)(2,1)S(1)}, u32[]{:S(2)}, u32[]{:S(2)}) collective-permute-start(bf16[128,128]{1,0:T(8,128)(2,1)S(1)} %get-tuple-element.69), channel_id=1, source_target_pairs={{0,249},{1,248},{2,251},{3,250},{4,253},{5,252},{6,255},{7,254},{8... | collective-permute-start | bytes 98312 | tf_op jit(solution)/shard_map/ppermute | solution.py:213
  10.4 15.6 %collective-permute-start.5 = (bf16[128,128]{1,0:T(8,128)(2,1)S(1)}, bf16[128,128]{1,0:T(8,128)(2,1)S(1)}, u32[]{:S(2)}, u32[]{:S(2)}) collective-permute-start(bf16[128,128]{1,0:T(8,128)(2,1)S(1)} %get-tuple-element.70), channel_id=1, source_target_pairs={{0,255},{1,250},{2,249},{3,252},{4,251},{5,254},{6,253},{7,248},{8... | collective-permute-start | bytes 98312 | tf_op jit(solution)/shard_map/ppermute | solution.py:213
  11.5 14.6 %collective-permute-start = (bf16[8,128,128]{2,1,0:T(8,128)(2,1)S(1)}, bf16[8,128,128]{2,1,0:T(8,128)(2,1)S(1)}, u32[]{:S(2)}, u32[]{:S(2)}) collective-permute-start(bf16[8,128,128]{2,1,0:T(8,128)(2,1)S(1)} %get-tuple-element.66), channel_id=1, source_target_pairs={{0,248},{1,249},{2,250},{3,251},{4,252},{5,253},{6,254},{7,255},{8... | collective-permute-start | bytes 786440 | tf_op jit(solution)/shard_map/ppermute | solution.py:213
  12.5 13.6 %collective-permute-start.6 = (bf16[8,128,128]{2,1,0:T(8,128)(2,1)S(1)}, bf16[8,128,128]{2,1,0:T(8,128)(2,1)S(1)}, u32[]{:S(2)}, u32[]{:S(2)}) collective-permute-start(bf16[8,128,128]{2,1,0:T(8,128)(2,1)S(1)} %get-tuple-element.71), channel_id=1, source_target_pairs={{0,8},{1,9},{2,10},{3,11},{4,12},{5,13},{6,14},{7,15},{8,0},{9,1},... | collective-permute-start | bytes 786440 | tf_op jit(solution)/shard_map/ppermute | solution.py:213
  19.2 6.8 %collective-permute-start.3 = (bf16[2,128,128]{2,1,0:T(8,128)(2,1)S(1)}, bf16[2,128,128]{2,1,0:T(8,128)(2,1)S(1)}, u32[]{:S(2)}, u32[]{:S(2)}) collective-permute-start(bf16[2,128,128]{2,1,0:T(8,128)(2,1)S(1)} %pad_maximum_fusion), channel_id=1, source_target_pairs={{0,8},{1,9},{2,10},{3,11},{4,12},{5,13},{6,14},{7,15},{8,0},{9,1},... | collective-permute-start | bytes 196616 | tf_op jit(solution)/shard_map/ppermute | solution.py:218
  19.3 0.7 copy-start.2
  26.1 9.6 %copy-start.1 = (bf16[4,8,128,128]{3,2,1,0:T(8,128)(2,1)S(1)}, bf16[4,8,128,128]{3,2,1,0:T(8,128)(2,1)}, u32[]{:S(2)}) copy-start(bf16[4,8,128,128]{3,2,1,0:T(8,128)(2,1)} %before.3) | copy-start | bytes 3145732
  27.5 13.7 %collective-permute-start.8 = (bf16[4,128,128]{2,1,0:T(8,128)(2,1)S(1)}, bf16[4,128,128]{2,1,0:T(8,128)(2,1)S(1)}, u32[]{:S(2)}, u32[]{:S(2)}) collective-permute-start(bf16[4,128,128]{2,1,0:T(8,128)(2,1)S(1)} %get-tuple-element.75), channel_id=1, source_target_pairs={{0,1},{1,0},{2,3},{3,2},{4,5},{5,4},{6,7},{7,6},{8,9},{9,8},{10,11... | collective-permute-start | bytes 393224 | tf_op jit(solution)/shard_map/ppermute | solution.py:213
  30.6 10.5 %collective-permute-start.9 = (bf16[4,128,128]{2,1,0:T(8,128)(2,1)S(1)}, bf16[4,128,128]{2,1,0:T(8,128)(2,1)S(1)}, u32[]{:S(2)}, u32[]{:S(2)}) collective-permute-start(bf16[4,128,128]{2,1,0:T(8,128)(2,1)S(1)} %get-tuple-element.76), channel_id=1, source_target_pairs={{0,7},{1,2},{2,1},{3,4},{4,3},{5,6},{6,5},{7,0},{8,15},{9,10},{10,... | collective-permute-start | bytes 393224 | tf_op jit(solution)/shard_map/ppermute | solution.py:213
  31.8 6.1 %collective-permute-start.10 = (bf16[128,128]{1,0:T(8,128)(2,1)S(1)}, bf16[128,128]{1,0:T(8,128)(2,1)S(1)}, u32[]{:S(2)}, u32[]{:S(2)}) collective-permute-start(bf16[128,128]{1,0:T(8,128)(2,1)S(1)} %get-tuple-element.77), channel_id=1, source_target_pairs={{0,249},{1,248},{2,251},{3,250},{4,253},{5,252},{6,255},{7,254},{8... | collective-permute-start | bytes 98312 | tf_op jit(solution)/shard_map/ppermute | solution.py:213
  31.8 9.3 %collective-permute-start.11 = (bf16[128,128]{1,0:T(8,128)(2,1)S(1)}, bf16[128,128]{1,0:T(8,128)(2,1)S(1)}, u32[]{:S(2)}, u32[]{:S(2)}) collective-permute-start(bf16[128,128]{1,0:T(8,128)(2,1)S(1)} %get-tuple-element.78), channel_id=1, source_target_pairs={{0,255},{1,250},{2,249},{3,252},{4,251},{5,254},{6,253},{7,248},{8... | collective-permute-start | bytes 98312 | tf_op jit(solution)/shard_map/ppermute | solution.py:213
  34.7 10.3 %collective-permute-start.7 = (bf16[8,128,128]{2,1,0:T(8,128)(2,1)S(1)}, bf16[8,128,128]{2,1,0:T(8,128)(2,1)S(1)}, u32[]{:S(2)}, u32[]{:S(2)}) collective-permute-start(bf16[8,128,128]{2,1,0:T(8,128)(2,1)S(1)} %get-tuple-element.74), channel_id=1, source_target_pairs={{0,248},{1,249},{2,250},{3,251},{4,252},{5,253},{6,254},{7,255},{8... | collective-permute-start | bytes 786440 | tf_op jit(solution)/shard_map/ppermute | solution.py:213
  37.9 7.1 %collective-permute-start.13 = (bf16[8,128,128]{2,1,0:T(8,128)(2,1)S(1)}, bf16[8,128,128]{2,1,0:T(8,128)(2,1)S(1)}, u32[]{:S(2)}, u32[]{:S(2)}) collective-permute-start(bf16[8,128,128]{2,1,0:T(8,128)(2,1)S(1)} %get-tuple-element.86), channel_id=1, source_target_pairs={{0,8},{1,9},{2,10},{3,11},{4,12},{5,13},{6,14},{7,15},{8,0},{9,1},... | collective-permute-start | bytes 786440 | tf_op jit(solution)/shard_map/ppermute | solution.py:213
  41.2 3.8 %collective-permute-start.12 = (bf16[2,128,128]{2,1,0:T(8,128)(2,1)S(1)}, bf16[2,128,128]{2,1,0:T(8,128)(2,1)S(1)}, u32[]{:S(2)}, u32[]{:S(2)}) collective-permute-start(bf16[2,128,128]{2,1,0:T(8,128)(2,1)S(1)} %pad_maximum_fusion.1), channel_id=1, source_target_pairs={{0,8},{1,9},{2,10},{3,11},{4,12},{5,13},{6,14},{7,15},{8,0},{9,1},... | collective-permute-start | bytes 196616 | tf_op jit(solution)/shard_map/ppermute | solution.py:218
  46.4 13.0 %collective-permute-start.15 = (bf16[4,128,128]{2,1,0:T(8,128)(2,1)S(1)}, bf16[4,128,128]{2,1,0:T(8,128)(2,1)S(1)}, u32[]{:S(2)}, u32[]{:S(2)}) collective-permute-start(bf16[4,128,128]{2,1,0:T(8,128)(2,1)S(1)} %get-tuple-element.92), channel_id=1, source_target_pairs={{0,1},{1,0},{2,3},{3,2},{4,5},{5,4},{6,7},{7,6},{8,9},{9,8},{10,11... | collective-permute-start | bytes 393224 | tf_op jit(solution)/shard_map/ppermute | solution.py:213
  48.2 11.2 %collective-permute-start.16 = (bf16[4,128,128]{2,1,0:T(8,128)(2,1)S(1)}, bf16[4,128,128]{2,1,0:T(8,128)(2,1)S(1)}, u32[]{:S(2)}, u32[]{:S(2)}) collective-permute-start(bf16[4,128,128]{2,1,0:T(8,128)(2,1)S(1)} %get-tuple-element.93), channel_id=1, source_target_pairs={{0,7},{1,2},{2,1},{3,4},{4,3},{5,6},{6,5},{7,0},{8,15},{9,10},{10,... | collective-permute-start | bytes 393224 | tf_op jit(solution)/shard_map/ppermute | solution.py:213
  49.7 5.9 %collective-permute-start.17 = (bf16[128,128]{1,0:T(8,128)(2,1)S(1)}, bf16[128,128]{1,0:T(8,128)(2,1)S(1)}, u32[]{:S(2)}, u32[]{:S(2)}) collective-permute-start(bf16[128,128]{1,0:T(8,128)(2,1)S(1)} %get-tuple-element.94), channel_id=1, source_target_pairs={{0,249},{1,248},{2,251},{3,250},{4,253},{5,252},{6,255},{7,254},{8... | collective-permute-start | bytes 98312 | tf_op jit(solution)/shard_map/ppermute | solution.py:213
  49.8 9.6 %collective-permute-start.18 = (bf16[128,128]{1,0:T(8,128)(2,1)S(1)}, bf16[128,128]{1,0:T(8,128)(2,1)S(1)}, u32[]{:S(2)}, u32[]{:S(2)}) collective-permute-start(bf16[128,128]{1,0:T(8,128)(2,1)S(1)} %get-tuple-element.95), channel_id=1, source_target_pairs={{0,255},{1,250},{2,249},{3,252},{4,251},{5,254},{6,253},{7,248},{8... | collective-permute-start | bytes 98312 | tf_op jit(solution)/shard_map/ppermute | solution.py:213
  52.8 10.4 %collective-permute-start.14 = (bf16[8,128,128]{2,1,0:T(8,128)(2,1)S(1)}, bf16[8,128,128]{2,1,0:T(8,128)(2,1)S(1)}, u32[]{:S(2)}, u32[]{:S(2)}) collective-permute-start(bf16[8,128,128]{2,1,0:T(8,128)(2,1)S(1)} %get-tuple-element.91), channel_id=1, source_target_pairs={{0,248},{1,249},{2,250},{3,251},{4,252},{5,253},{6,254},{7,255},{8... | collective-permute-start | bytes 786440 | tf_op jit(solution)/shard_map/ppermute | solution.py:213
  55.6 7.7 %collective-permute-start.20 = (bf16[8,128,128]{2,1,0:T(8,128)(2,1)S(1)}, bf16[8,128,128]{2,1,0:T(8,128)(2,1)S(1)}, u32[]{:S(2)}, u32[]{:S(2)}) collective-permute-start(bf16[8,128,128]{2,1,0:T(8,128)(2,1)S(1)} %get-tuple-element.104), channel_id=1, source_target_pairs={{0,8},{1,9},{2,10},{3,11},{4,12},{5,13},{6,14},{7,15},{8,0},{9,1},... | collective-permute-start | bytes 786440 | tf_op jit(solution)/shard_map/ppermute | solution.py:213
  59.4 3.8 %collective-permute-start.19 = (bf16[2,128,128]{2,1,0:T(8,128)(2,1)S(1)}, bf16[2,128,128]{2,1,0:T(8,128)(2,1)S(1)}, u32[]{:S(2)}, u32[]{:S(2)}) collective-permute-start(bf16[2,128,128]{2,1,0:T(8,128)(2,1)S(1)} %pad_maximum_fusion.2), channel_id=1, source_target_pairs={{0,8},{1,9},{2,10},{3,11},{4,12},{5,13},{6,14},{7,15},{8,0},{9,1},... | collective-permute-start | bytes 196616 | tf_op jit(solution)/shard_map/ppermute | solution.py:218
  64.6 13.7 %collective-permute-start.22 = (bf16[4,128,128]{2,1,0:T(8,128)(2,1)S(1)}, bf16[4,128,128]{2,1,0:T(8,128)(2,1)S(1)}, u32[]{:S(2)}, u32[]{:S(2)}) collective-permute-start(bf16[4,128,128]{2,1,0:T(8,128)(2,1)S(1)} %get-tuple-element.110), channel_id=1, source_target_pairs={{0,1},{1,0},{2,3},{3,2},{4,5},{5,4},{6,7},{7,6},{8,9},{9,8},{10,11... | collective-permute-start | bytes 393224 | tf_op jit(solution)/shard_map/ppermute | solution.py:213
  64.9 13.3 %collective-permute-start.23 = (bf16[4,128,128]{2,1,0:T(8,128)(2,1)S(1)}, bf16[4,128,128]{2,1,0:T(8,128)(2,1)S(1)}, u32[]{:S(2)}, u32[]{:S(2)}) collective-permute-start(bf16[4,128,128]{2,1,0:T(8,128)(2,1)S(1)} %get-tuple-element.111), channel_id=1, source_target_pairs={{0,7},{1,2},{2,1},{3,4},{4,3},{5,6},{6,5},{7,0},{8,15},{9,10},{10,... | collective-permute-start | bytes 393224 | tf_op jit(solution)/shard_map/ppermute | solution.py:213
  68.4 5.2 %collective-permute-start.24 = (bf16[128,128]{1,0:T(8,128)(2,1)S(1)}, bf16[128,128]{1,0:T(8,128)(2,1)S(1)}, u32[]{:S(2)}, u32[]{:S(2)}) collective-permute-start(bf16[128,128]{1,0:T(8,128)(2,1)S(1)} %get-tuple-element.112), channel_id=1, source_target_pairs={{0,249},{1,248},{2,251},{3,250},{4,253},{5,252},{6,255},{7,254},{8... | collective-permute-start | bytes 98312 | tf_op jit(solution)/shard_map/ppermute | solution.py:213
  68.5 9.8 %collective-permute-start.25 = (bf16[128,128]{1,0:T(8,128)(2,1)S(1)}, bf16[128,128]{1,0:T(8,128)(2,1)S(1)}, u32[]{:S(2)}, u32[]{:S(2)}) collective-permute-start(bf16[128,128]{1,0:T(8,128)(2,1)S(1)} %get-tuple-element.113), channel_id=1, source_target_pairs={{0,255},{1,250},{2,249},{3,252},{4,251},{5,254},{6,253},{7,248},{8... | collective-permute-start | bytes 98312 | tf_op jit(solution)/shard_map/ppermute | solution.py:213
  71.4 10.4 %collective-permute-start.21 = (bf16[8,128,128]{2,1,0:T(8,128)(2,1)S(1)}, bf16[8,128,128]{2,1,0:T(8,128)(2,1)S(1)}, u32[]{:S(2)}, u32[]{:S(2)}) collective-permute-start(bf16[8,128,128]{2,1,0:T(8,128)(2,1)S(1)} %get-tuple-element.109), channel_id=1, source_target_pairs={{0,248},{1,249},{2,250},{3,251},{4,252},{5,253},{6,254},{7,255},{8... | collective-permute-start | bytes 786440 | tf_op jit(solution)/shard_map/ppermute | solution.py:213
  73.7 8.1 %collective-permute-start.27 = (bf16[8,128,128]{2,1,0:T(8,128)(2,1)S(1)}, bf16[8,128,128]{2,1,0:T(8,128)(2,1)S(1)}, u32[]{:S(2)}, u32[]{:S(2)}) collective-permute-start(bf16[8,128,128]{2,1,0:T(8,128)(2,1)S(1)} %get-tuple-element.120), channel_id=1, source_target_pairs={{0,8},{1,9},{2,10},{3,11},{4,12},{5,13},{6,14},{7,15},{8,0},{9,1},... | collective-permute-start | bytes 786440 | tf_op jit(solution)/shard_map/ppermute | solution.py:213
  78.3 3.5 %collective-permute-start.26 = (bf16[2,128,128]{2,1,0:T(8,128)(2,1)S(1)}, bf16[2,128,128]{2,1,0:T(8,128)(2,1)S(1)}, u32[]{:S(2)}, u32[]{:S(2)}) collective-permute-start(bf16[2,128,128]{2,1,0:T(8,128)(2,1)S(1)} %pad_maximum_fusion.3), channel_id=1, source_target_pairs={{0,8},{1,9},{2,10},{3,11},{4,12},{5,13},{6,14},{7,15},{8,0},{9,1},... | collective-permute-start | bytes 196616 | tf_op jit(solution)/shard_map/ppermute | solution.py:218
